TPU v7x, 512 devices: a whole 4x8x8 slice. The times are simulated.
512 devices in a mesh: dp: 16 (over y, core), seq: 32 (over z, x).
Axes of the slice: x: 4, y: 8, z: 8, core: 2. Of those that a mesh axis runs over, the one named last changes fastest.
Arguments:
- query_rows: bfloat16 [2048, 32, 2048], P('seq', 'dp'), may hold values from -6 to 6
- key_rows: bfloat16 [2048, 32, 2048], P('seq', 'dp'), may hold values from -6 to 6
- value_rows: bfloat16 [2048, 32, 2048], P('seq', 'dp'), may hold values from -6 to 6
- region_lengths: int32 [32], P('dp'), may hold values from 256 to 2048, as said below
- norm_gain: float32 [2048], replicated, may hold values from 0.1 to 1.9
- conv_weight: bfloat16 [9, 128, 128], replicated, may hold values from -0.1875 to 0.1875
- cotangent: bfloat16 [32, 128, 256, 128], P('dp', 'seq'), may hold values from -6 to 6
Outputs:
- decoded: bfloat16 [32, 128, 256, 128], P('dp', 'seq')
- weight_grad: float32 [9, 128, 128], replicated
Inputs may be any that keep to these rules, and one draw needn't show every extreme that they name: Region r's tokens fill its first region_lengths[r] slots; in every draw some region fills all 2048 slots.
All inputs are finite; a program needn't handle non-finite values.
Results may differ from a plain program's by a relative error of at most 0.0063.
Values may be sent and summed in bfloat16 or wider, within the bound.
A program may use at most 64 MiB of HBM per device.

v0:
```python
import math

import jax
import jax.numpy as jnp
from jax import lax
from jax.sharding import PartitionSpec as P

HEADS = 16
PATCH = 4


def extended(shard, sides, width):
    for axis, dim in sides:
        size, length = (lax.axis_size(axis), shard.shape[dim])
        up = [(i, (i + 1) % size) for i in range(size - 1)]
        down = [(j, i) for i, j in up]
        last = lax.slice_in_dim(shard, length - width, length, axis=dim)
        initial = lax.slice_in_dim(shard, 0, width, axis=dim)
        before = lax.ppermute(last, axis, up)
        after = lax.ppermute(initial, axis, down)
        shard = jnp.concatenate([before, shard, after], axis=dim)
    return shard


def attend(query_mat, key_mat, value_mat, live_rows, key_count):
    total_rows = query_mat.shape[0]
    block_rows = min(512, total_rows)
    scale_factor = 1.0 / math.sqrt(query_mat.shape[1])
    key_valid = jnp.arange(key_mat.shape[0], dtype=jnp.int32) < key_count

    def one_block(number, output):
        start_row = number * block_rows
        query_blk = lax.dynamic_slice_in_dim(query_mat, start_row, block_rows, 0)
        scores = (
            lax.dot_general(
                query_blk, key_mat, (((1,), (1,)), ((), ())), preferred_element_type=jnp.float32
            )
            * scale_factor
        )
        scores = jnp.where(key_valid[None, :], scores, -1e30)
        top_score = jnp.max(scores, axis=1, keepdims=True)
        powers = jnp.exp(scores - top_score)
        totals = jnp.sum(powers, axis=1, keepdims=True)
        mixed = (
            jnp.dot(powers.astype(jnp.bfloat16), value_mat, preferred_element_type=jnp.float32)
            / totals
        )
        return lax.dynamic_update_slice_in_dim(output, mixed.astype(jnp.bfloat16), start_row, 0)

    blocks_live = (live_rows + block_rows - 1) // block_rows
    return lax.fori_loop(0, blocks_live, one_block, jnp.zeros(query_mat.shape, jnp.bfloat16))


def pick_length(lengths_local, which):
    return jnp.sum(
        jnp.where(jnp.arange(lengths_local.shape[0], dtype=jnp.int32) == which, lengths_local, 0)
    )


def body(query_rows, key_rows, value_rows, region_lengths, norm_gain, conv_weight, cotangent):
    local_tokens, group_regions, model_width = query_rows.shape
    head_width = model_width // HEADS
    seq_count = lax.axis_size("seq")
    seq_index = lax.axis_index("seq")
    item_total = group_regions * HEADS
    got_query, got_key, got_value = (
        lax.all_to_all(
            query_rows.reshape(local_tokens, item_total, head_width),
            "seq",
            split_axis=1,
            concat_axis=0,
            tiled=True,
        ),
        lax.all_to_all(
            key_rows.reshape(local_tokens, item_total, head_width),
            "seq",
            split_axis=1,
            concat_axis=0,
            tiled=True,
        ),
        lax.all_to_all(
            value_rows.reshape(local_tokens, item_total, head_width),
            "seq",
            split_axis=1,
            concat_axis=0,
            tiled=True,
        ),
    )
    per_device = item_total // seq_count
    global_item = seq_index * per_device + 0
    region_len = pick_length(region_lengths, global_item // HEADS)
    outputs = [attend(got_query[:, 0], got_key[:, 0], got_value[:, 0], region_len, region_len)]
    stacked = jnp.stack(outputs, axis=1)
    returned = lax.all_to_all(stacked, "seq", split_axis=0, concat_axis=1, tiled=True)
    attended = returned.reshape(local_tokens, group_regions, model_width)
    values32 = attended.astype(jnp.float32)
    mean_val = jnp.mean(values32, axis=-1, keepdims=True)
    centered = values32 - mean_val
    variance = jnp.mean(centered * centered, axis=-1, keepdims=True)
    normed = centered * lax.rsqrt(variance + 1e-05) * norm_gain
    positions = seq_index * local_tokens + jnp.arange(local_tokens, dtype=jnp.int32)
    token_live = positions[:, None] < region_lengths[None, :]
    normed = jnp.where(token_live[:, :, None], normed, 0.0).astype(jnp.bfloat16)
    channels = model_width // (PATCH * PATCH)
    pix_cols = local_tokens * PATCH
    image = normed.reshape(local_tokens, group_regions, PATCH, PATCH, channels).transpose(
        1, 2, 0, 3, 4
    )
    image = image.reshape(group_regions, PATCH, pix_cols, channels)
    rimmed = extended(image, (("seq", 1),), 1)
    padded = jnp.pad(rimmed, ((0, 0), (0, 0), (1, 1), (0, 0)))
    cot_flat = cotangent.reshape(-1, channels)
    accum = jnp.zeros((group_regions * PATCH * pix_cols, channels), jnp.float32)
    grads = []
    for tap_number in range(9):
        row_shift, col_shift = divmod(tap_number, 3)
        window = padded[
            :, row_shift : row_shift + PATCH, col_shift : col_shift + pix_cols, :
        ].reshape(-1, channels)
        accum = accum + jnp.dot(window, conv_weight[tap_number], preferred_element_type=jnp.float32)
        grads.append(jnp.dot(window.T, cot_flat, preferred_element_type=jnp.float32))
    decoded = accum.reshape(cotangent.shape).astype(jnp.bfloat16)
    local_grad = jnp.stack(grads)
    factor = 1.0 / math.sqrt(PATCH * pix_cols)
    summed = lax.psum(local_grad, ("dp", "seq"))
    return (decoded, summed * factor)


def solution(mesh):
    placed = (
        P("seq", "dp", None),
        P("seq", "dp", None),
        P("seq", "dp", None),
        P("dp"),
        P(),
        P(),
        P("dp", "seq", None, None),
    )
    return jax.shard_map(
        body,
        mesh=mesh,
        in_specs=placed,
        out_specs=(P("dp", "seq", None, None), P()),
        check_vma=False,
    )
```

profile of v0, /device:TPU:1, one launch (start us, length us, event | category | flops | bytes accessed | tf_op | source)
XLA Modules:
  0.0 426.8 jit_solution(7889504332392062403)
XLA Ops:
  7.2 1.5 reshape.111
  8.7 1.0 copy.50
  9.7 13.7 %all-to-all-start = ((bf16[64,32,128]{2,0,1:T(8,128)(2,1)}), bf16[64,32,128]{2,0,1:T(8,128)(2,1)S(1)}, u32[]{:S(2)}, u32[]{:S(2)}) async-start(bf16[64,32,128]{2,0,1:T(8,128)(2,1)} %copy.50), calls=%async_computation | async-start | bytes 1048576 | tf_op jit(solution)/shard_map/all_to_all | solution.py:67
  23.4 0.3 reshape.112
  23.7 1.0 copy.51
  24.7 14.9 %all-to-all-done = bf16[64,32,128]{2,0,1:T(8,128)(2,1)S(1)} async-done(((bf16[64,32,128]{2,0,1:T(8,128)(2,1)}), bf16[64,32,128]{2,0,1:T(8,128)(2,1)S(1)}, u32[]{:S(2)}, u32[]{:S(2)}) %all-to-all-start) | async-done | bytes 524320 | tf_op jit(solution)/shard_map/all_to_all | solution.py:67
  39.7 5.3 %all-to-all-start.1 = ((bf16[64,32,128]{2,0,1:T(8,128)(2,1)}), bf16[64,32,128]{2,0,1:T(8,128)(2,1)S(1)}, u32[]{:S(2)}, u32[]{:S(2)}) async-start(bf16[64,32,128]{2,0,1:T(8,128)(2,1)} %copy.51), calls=%async_computation.1 | async-start | bytes 1048576 | tf_op jit(solution)/shard_map/all_to_all | solution.py:74
  45.3 1.0 copy.52
  46.3 13.9 %all-to-all-done.1 = bf16[64,32,128]{2,0,1:T(8,128)(2,1)S(1)} async-done(((bf16[64,32,128]{2,0,1:T(8,128)(2,1)}), bf16[64,32,128]{2,0,1:T(8,128)(2,1)S(1)}, u32[]{:S(2)}, u32[]{:S(2)}) %all-to-all-start.1) | async-done | bytes 524320 | tf_op jit(solution)/shard_map/all_to_all | solution.py:74
  60.2 6.3 %all-to-all-start.2 = ((bf16[64,32,128]{2,0,1:T(8,128)(2,1)}), bf16[64,32,128]{2,0,1:T(8,128)(2,1)S(1)}, u32[]{:S(2)}, u32[]{:S(2)}) async-start(bf16[64,32,128]{2,0,1:T(8,128)(2,1)} %copy.52), calls=%async_computation.2 | async-start | bytes 1048576 | tf_op jit(solution)/shard_map/all_to_all | solution.py:81
  66.5 0.7 fusion.64
  67.9 13.8 %all-to-all-done.2 = bf16[64,32,128]{2,0,1:T(8,128)(2,1)S(1)} async-done(((bf16[64,32,128]{2,0,1:T(8,128)(2,1)}), bf16[64,32,128]{2,0,1:T(8,128)(2,1)S(1)}, u32[]{:S(2)}, u32[]{:S(2)}) %all-to-all-start.2) | async-done | bytes 524320 | tf_op jit(solution)/shard_map/all_to_all | solution.py:81
  81.7 10.7 %while.11 = (s32[]{:T(128)}, bf16[2048,128]{1,0:T(8,128)(2,1)S(1)}, s32[]{:T(128)}, bf16[2048,128]{1,0:T(8,128)(2,1)S(1)}, bf16[2048,128]{1,0:T(8,128)(2,1)S(1)}...) while((s32[]{:T(128)}, bf16[2048,128]{1,0:T(8,128)(2,1)S(1)}, ...), condition=%wide.region_4.5_spmd.clone, body=%wide.region_1.4_spmd.clone.sunk | while | flops 548537344 | bytes 13912231 | solution.py:51
  81.8 0.7 iota_compare_fusion.4
  82.5 0.8 fusion.105
  83.3 0.9 fusion.106
  84.3 1.1 fusion.107
  85.3 0.7 iota_compare_fusion.4
  86.0 0.8 fusion.105
  86.9 0.9 fusion.106
  87.8 1.0 fusion.107
  88.9 0.7 iota_compare_fusion.4
  89.6 0.8 fusion.105
  90.5 0.9 fusion.106
  91.4 1.1 fusion.107
  92.5 0.5 broadcast.85
  93.0 1.0 reduce.4
  94.0 0.9 reshape.136
  94.9 9.9 %all-to-all-start.3 = ((bf16[32,2,4096]{2,1,0:T(2,128)(2,1)}), bf16[32,2,4096]{2,1,0:T(2,128)(2,1)S(1)}, u32[]{:S(2)}, u32[]{:S(2)}) async-start(bf16[32,2,4096]{2,1,0:T(2,128)(2,1)} %reshape.136), calls=%async_computation.3 | async-start | bytes 1048576 | tf_op jit(solution)/shard_map/all_to_all | solution.py:94
  105.0 12.5 %all-to-all-done.3 = bf16[32,2,4096]{2,1,0:T(2,128)(2,1)S(1)} async-done(((bf16[32,2,4096]{2,1,0:T(2,128)(2,1)}), bf16[32,2,4096]{2,1,0:T(2,128)(2,1)S(1)}, u32[]{:S(2)}, u32[]{:S(2)}) %all-to-all-start.3) | async-done | bytes 524320 | tf_op jit(solution)/shard_map/all_to_all | solution.py:94
  117.5 0.5 reshape.137
  118.0 1.1 convert_element_type.49
  119.2 0.3 reduce_sum.44
  119.6 0.6 multiply_reduce_fusion
  120.5 0.4 copy.54
  121.2 2.2 collective-permute-start
  123.4 1.5 collective-permute-start.1
  124.9 0.4 collective-permute-done
  125.3 3.8 collective-permute-done.1
  129.1 0.6 fusion.28
  129.8 1.8 fusion.73
  131.6 0.9 fusion.37
  132.5 0.9 fusion.30
  133.4 1.0 fusion.36
  134.4 0.9 fusion.35
  135.4 1.0 fusion.34
  136.3 1.0 fusion.33
  137.3 0.9 fusion.32
  138.3 0.9 fusion.29
  139.2 1.0 fusion.31
  140.2 1.1 pad_maximum_fusion
  141.3 2.1 copy.60
  143.3 2.0 copy.58
  145.4 2.1 copy.61
  147.4 1.0 copy.62
  148.4 1.0 copy.64
  149.5 1.0 copy.65
  150.5 1.0 copy.67
  152.1 0.5 copy-done.9
  153.5 0.5 copy-done.6
  154.5 0.5 copy-done.5
  155.6 1.1 fusion.22
  156.7 261.3 %all-reduce.3.cloned.1.call-done = f32[9,128,128]{2,1,0:T(8,128)} async-done(((f32[9,128,128]{2,1,0:T(8,128)}), f32[9,128,128]{2,1,0:T(8,128)}) %all-reduce.3.cloned.1.call-update) | async-done | bytes 589840 | tf_op jit(solution)/shard_map/psum | solution.py:125
  418.0 1.9 broadcast_multiply_fusion
  (50 shorter events, 3.7 us)
Async XLA Ops:
  7.2 124.4 %copy-start = (bf16[2,4,256,128]{3,2,1,0:T(8,128)(2,1)S(1)}, bf16[2,4,256,128]{3,2,1,0:T(8,128)(2,1)}, u32[]{:S(2)}) copy-start(bf16[2,4,256,128]{3,2,1,0:T(8,128)(2,1)} %param.15) | copy-start | bytes 1572868
  7.2 16.2 %copy-start.10 = (bf16[64,2,2048]{2,1,0:T(2,128)(2,1)S(1)}, bf16[64,2,2048]{2,1,0:T(2,128)(2,1)}, u32[]{:S(2)}) copy-start(bf16[64,2,2048]{2,1,0:T(2,128)(2,1)} %param.10) | copy-start | bytes 1572868
  8.7 36.3 %copy-start.11 = (bf16[64,2,2048]{2,1,0:T(2,128)(2,1)S(1)}, bf16[64,2,2048]{2,1,0:T(2,128)(2,1)}, u32[]{:S(2)}) copy-start(bf16[64,2,2048]{2,1,0:T(2,128)(2,1)} %param.11) | copy-start | bytes 1572868
  9.7 30.0 %all-to-all-start = ((bf16[64,32,128]{2,0,1:T(8,128)(2,1)}), bf16[64,32,128]{2,0,1:T(8,128)(2,1)S(1)}, u32[]{:S(2)}, u32[]{:S(2)}) async-start(bf16[64,32,128]{2,0,1:T(8,128)(2,1)} %copy.50), calls=%async_computation | async-start | bytes 1048576 | tf_op jit(solution)/shard_map/all_to_all | solution.py:67
  24.7 41.8 %copy-start.14 = (s32[2]{0:T(128)S(1)}, s32[2]{0:T(128)}, u32[]{:S(2)}) copy-start(s32[2]{0:T(128)} %param.12) | copy-start | bytes 28
  39.7 20.5 %all-to-all-start.1 = ((bf16[64,32,128]{2,0,1:T(8,128)(2,1)}), bf16[64,32,128]{2,0,1:T(8,128)(2,1)S(1)}, u32[]{:S(2)}, u32[]{:S(2)}) async-start(bf16[64,32,128]{2,0,1:T(8,128)(2,1)} %copy.51), calls=%async_computation.1 | async-start | bytes 1048576 | tf_op jit(solution)/shard_map/all_to_all | solution.py:74
  60.2 21.5 %all-to-all-start.2 = ((bf16[64,32,128]{2,0,1:T(8,128)(2,1)}), bf16[64,32,128]{2,0,1:T(8,128)(2,1)S(1)}, u32[]{:S(2)}, u32[]{:S(2)}) async-start(bf16[64,32,128]{2,0,1:T(8,128)(2,1)} %copy.52), calls=%async_computation.2 | async-start | bytes 1048576 | tf_op jit(solution)/shard_map/all_to_all | solution.py:81
  94.9 22.6 %all-to-all-start.3 = ((bf16[32,2,4096]{2,1,0:T(2,128)(2,1)}), bf16[32,2,4096]{2,1,0:T(2,128)(2,1)S(1)}, u32[]{:S(2)}, u32[]{:S(2)}) async-start(bf16[32,2,4096]{2,1,0:T(2,128)(2,1)} %reshape.136), calls=%async_computation.3 | async-start | bytes 1048576 | tf_op jit(solution)/shard_map/all_to_all | solution.py:94
  104.8 313.2 %all-reduce.3.cloned.1.call-start = ((), (), s32[]{:S(2)}) async-start(), calls=%async_computation.4 | async-start | bytes 1179648 | tf_op jit(solution)/shard_map/psum | solution.py:125
  118.0 2.2 copy-start.13
  121.2 4.1 collective-permute-start
  123.4 5.7 %collective-permute-start.1 = (bf16[2,1,256,128]{2,3,1,0:T(8,128)(2,1)S(1)}, bf16[2,1,256,128]{2,3,1,0:T(8,128)(2,1)S(1)}, u32[]{:S(2)}, u32[]{:S(2)}) collective-permute-start(bf16[2,1,256,128]{2,3,1,0:T(8,128)(2,1)S(1)} %get-tuple-element.84), channel_id=1, source_target_pairs={{1,0},{2,1},{3,2},{4,3},{5,4},{6,5},{7,6},{8,7},{9,8},{10,9},{11,1... | collective-permute-start | bytes 393224 | tf_op jit(solution)/shard_map/ppermute | solution.py:20
  141.3 6.2 %copy-start.1 = (bf16[2,4,256,128]{2,3,1,0:T(8,128)(2,1)S(1)}, bf16[2,4,256,128]{2,3,1,0:T(8,128)(2,1)}, u32[]{:S(2)}) copy-start(bf16[2,4,256,128]{2,3,1,0:T(8,128)(2,1)} %get-tuple-element.78) | copy-start | bytes 1572868
  147.4 4.1 copy-start.12
  148.4 2.1 copy-start.2
  149.5 2.0 copy-start.3
  150.5 1.3 copy-start.7
  151.5 1.1 copy-start.9
  151.8 1.1 copy-start.8
  152.9 1.0 copy-start.6
  153.2 1.1 copy-start.4
  153.9 1.1 copy-start.5
Sparse Core Ops, SparseCore 0:
  140.3 277.6 all-reduce.2
where the time goes:
time: 428 us; the launch traced here: 427 us
  waiting for transfers between devices  321 us (75%)
  starting transfers between devices  38.9 us (9%)
  local copies, waits for them, and re-layouts  21.7 us (5%)
  matrix products  17.5 us (4%)
  between operations  15.1 us (4%)
  other arithmetic  12.8 us (3%)
    psum x1, waiting for transfers between devices, body(): summed = lax.psum(local_grad, ('dp', 'seq'))  261 us
    all_to_all x1, waiting for transfers between devices, body(): lax.all_to_all(query_rows.reshape(local_tokens, item_total, head_width),...  14.9 us
    all_to_all x1, waiting for transfers between devices, body(): lax.all_to_all(key_rows.reshape(local_tokens, item_total, head_width), 's...  13.9 us
    all_to_all x1, waiting for transfers between devices, body(): lax.all_to_all(value_rows.reshape(local_tokens, item_total, head_width),...  13.8 us
    all_to_all x1, starting transfers between devices, body(): lax.all_to_all(query_rows.reshape(local_tokens, item_total, head_width),...  13.7 us
    all_to_all x1, waiting for transfers between devices, body(): lax.all_to_all(stacked, 'seq', split_axis=0, concat_axis=1, tiled=True)  12.5 us
    slice x9, local copies, waits for them, and re-layouts, body(): padded[:, row_shift:row_shift + PATCH, col_shift:col_shift + pix_cols, :]  12.3 us
    all_to_all x1, starting transfers between devices, body(): lax.all_to_all(stacked, 'seq', split_axis=0, concat_axis=1, tiled=True)  9.89 us
  transfers between devices with their start and end apart: 7, of which 7 were waited for; matrix products, arithmetic and copies ran while one was open for 4% of the time, Pallas kernels for 0%

commit v1 on v0

--- a/solution.py
+++ b/solution.py
@@ -1,12 +1,139 @@
+import functools
 import math
 
 import jax
 import jax.numpy as jnp
 from jax import lax
+from jax.experimental import pallas as pl
+from jax.experimental.pallas import tpu as pltpu
 from jax.sharding import PartitionSpec as P
 
 HEADS = 16
 PATCH = 4
+MESH = pl.DeviceIdType.MESH
+X = 4
+OWNED = 18
+
+
+def reduce_kernel(n_dp, n_seq, g_ref, out_ref, buf1, acc1, buf2, acc2, buf3, fin,
+                  s1, r1, s2, r2, s3, r3, s4, r4, s5, r5, s6, r6):
+    dp, seq = lax.axis_index("dp"), lax.axis_index("seq")
+    n_z = n_seq // X
+    n_yz = (n_dp // 2) * n_z
+    core, x = dp % 2, seq % X
+    member = (dp // 2) * n_z + seq // X
+    partner = (dp + 1 - 2 * core, seq)
+
+    def x_peer(step):
+        return (dp, seq - x + (x + step) % X)
+
+    def yz_device(index):
+        return ((index // n_z) * 2 + core, (index % n_z) * X + x)
+
+    barrier = pltpu.get_barrier_semaphore()
+    pl.semaphore_signal(barrier, inc=1, device_id=partner, device_id_type=MESH)
+    for step in range(1, X):
+        pl.semaphore_signal(barrier, inc=1, device_id=x_peer(step), device_id_type=MESH)
+
+    def greet(step, _):
+        pl.semaphore_signal(barrier, inc=1, device_id=yz_device((member + step) % n_yz), device_id_type=MESH)
+        return 0
+
+    lax.fori_loop(1, n_yz, greet, 0)
+    pl.semaphore_wait(barrier, 1 + (X - 1) + (n_yz - 1))
+
+    def remote(src, dst, send, recv, device):
+        return pltpu.make_async_remote_copy(src_ref=src, dst_ref=dst, send_sem=send, recv_sem=recv,
+                                            device_id=device, device_id_type=MESH)
+
+    swap = remote(g_ref.at[:, pl.ds(8 * (1 - core), 8)], buf1, s1, r1, partner)
+    swap.start()
+    swap.wait()
+    acc1[...] = g_ref[:, pl.ds(8 * core, 8)] + buf1[...]
+    copies = []
+    for step in range(1, X):
+        to = (x + step) % X
+        copy = remote(acc1.at[:, pl.ds(2 * to, 2)], buf2.at[step - 1], s2.at[step - 1], r2.at[step - 1], x_peer(step))
+        copy.start()
+        copies.append(copy)
+    for copy in copies:
+        copy.wait()
+    acc2[...] = (acc1[:, pl.ds(2 * x, 2)] + buf2[0]) + (buf2[1] + buf2[2])
+    turned = (member + n_yz - core) % n_yz
+    for tile in range(OWNED):
+        owner = (3 * tile + core) % n_yz
+
+        @pl.when(owner != member)
+        def _():
+            remote(acc2.at[tile // 2, tile % 2], buf3.at[member], s3, r3, yz_device(owner)).start()
+
+    mine = turned // 3
+    owns = jnp.logical_and(turned % 3 == 0, mine < OWNED)
+
+    def wait_bytes(ref, sem):
+        pltpu.make_async_copy(ref, ref, sem).wait()
+
+    @pl.when(owns)
+    def _():
+        wait_bytes(buf3.at[pl.ds(0, OWNED - 1)], s3)
+        wait_bytes(buf3.at[pl.ds(0, n_yz - 1)], r3)
+        buf3[member] = acc2[mine // 2, mine % 2]
+        fin[mine // 2, mine % 2] = jnp.sum(buf3[...], axis=0) * (1.0 / 32.0)
+        part = fin.at[mine // 2, mine % 2]
+
+        def spread(step, _):
+            remote(part, part, s4, r4, yz_device((member + step) % n_yz)).start()
+            return 0
+
+        lax.fori_loop(1, n_yz, spread, 0)
+        wait_bytes(buf3.at[pl.ds(0, n_yz - 1)], s4)
+        wait_bytes(buf3.at[pl.ds(0, OWNED - 1)], r4)
+
+    @pl.when(jnp.logical_not(owns))
+    def _():
+        wait_bytes(buf3.at[pl.ds(0, OWNED)], s3)
+        wait_bytes(buf3.at[pl.ds(0, OWNED)], r4)
+
+    def place(which):
+        return out_ref.at[:, pl.ds(8 * core + 2 * which, 2)]
+
+    copies = []
+    for step in range(1, X):
+        copy = remote(fin, place(x), s5.at[step - 1], r5.at[step - 1], x_peer(step))
+        copy.start()
+        copies.append(copy)
+    out_ref[:, pl.ds(8 * core + 2 * x, 2)] = fin[...]
+    forwards = [remote(fin, place(x), s6.at[0], r6.at[0], partner)]
+    forwards[0].start()
+    for step in range(1, X):
+        copies[step - 1].wait()
+        came = place((x + X - step) % X)
+        forward = remote(came, came, s6.at[step], r6.at[step], partner)
+        forward.start()
+        forwards.append(forward)
+    for forward in forwards:
+        forward.wait()
+
+
+def all_sum(grads, n_dp, n_seq):
+    f32 = jnp.float32
+    n_yz = (n_dp // 2) * (n_seq // X)
+    dma = pltpu.SemaphoreType.DMA
+    out = pl.pallas_call(
+        functools.partial(reduce_kernel, n_dp, n_seq),
+        out_shape=jax.ShapeDtypeStruct((9, 16, 8, 128), f32),
+        in_specs=[pl.BlockSpec(memory_space=pltpu.VMEM)],
+        out_specs=pl.BlockSpec(memory_space=pltpu.VMEM),
+        scratch_shapes=[
+            pltpu.VMEM((9, 8, 8, 128), f32), pltpu.VMEM((9, 8, 8, 128), f32),
+            pltpu.VMEM((3, 9, 2, 8, 128), f32), pltpu.VMEM((9, 2, 8, 128), f32),
+            pltpu.VMEM((n_yz, 8, 128), f32), pltpu.VMEM((9, 2, 8, 128), f32),
+            dma, dma, dma((3,)), dma((3,)), dma, dma, dma, dma, dma((3,)), dma((3,)), dma((4,)), dma((4,)),
+        ],
+        compiler_params=pltpu.CompilerParams(collective_id=0, has_side_effects=True),
+        name="reduce_all",
+    )(grads.reshape(9, 16, 8, 128))
+    return out.reshape(9, 128, 128)
 
 
 def extended(shard, sides, width):
@@ -121,9 +248,8 @@
         grads.append(jnp.dot(window.T, cot_flat, preferred_element_type=jnp.float32))
     decoded = accum.reshape(cotangent.shape).astype(jnp.bfloat16)
     local_grad = jnp.stack(grads)
-    factor = 1.0 / math.sqrt(PATCH * pix_cols)
-    summed = lax.psum(local_grad, ("dp", "seq"))
-    return (decoded, summed * factor)
+    summed = all_sum(local_grad, lax.axis_size("dp"), seq_count)
+    return (decoded, summed)
 
 
 def solution(mesh):

time: 428 us -> 200 us (0.47)
  waiting for transfers between devices: 321 us -> 62.6 us
  Pallas kernels: 0 us -> 43.3 us
  between operations: 15.1 us -> 1.74 us
    psum x1 -> x0, waiting for transfers between devices: 261 us -> none  [body(): summed = lax.psum(local_grad, ('dp', 'seq'))]
    pallas_call x0 -> x1, Pallas kernels: none -> 43.3 us  [all_sum(): pl.pallas_call(functools.partial(reduce_kernel, n_dp, n_seq), out_shape=j...]
  transfers between devices with their start and end apart: 7 -> 6, of which waited for: 7 -> 5; matrix products, arithmetic and copies ran while one was open for 4% -> 2% of each run, Pallas kernels for 0% -> 0%
where the time goes in v1:
time: 200 us; the launch traced here: 198 us
  waiting for transfers between devices  62.6 us (31%)
  Pallas kernels  43.3 us (22%)
  starting transfers between devices  39.1 us (20%)
  local copies, waits for them, and re-layouts  21.8 us (11%)
  matrix products  18.6 us (9%)
  other arithmetic  10.9 us (5%)
    pallas_call x1, Pallas kernels, all_sum(): pl.pallas_call(functools.partial(reduce_kernel, n_dp, n_seq), out_shape=j...  43.3 us
    all_to_all x1, waiting for transfers between devices, body(): lax.all_to_all(stacked, 'seq', split_axis=0, concat_axis=1, tiled=True)  16 us
    all_to_all x1, waiting for transfers between devices, body(): lax.all_to_all(query_rows.reshape(local_tokens, item_total, head_width),...  14.9 us
    all_to_all x1, waiting for transfers between devices, body(): lax.all_to_all(key_rows.reshape(local_tokens, item_total, head_width), 's...  13.9 us
    all_to_all x1, waiting for transfers between devices, body(): lax.all_to_all(value_rows.reshape(local_tokens, item_total, head_width),...  13.8 us
    all_to_all x1, starting transfers between devices, body(): lax.all_to_all(query_rows.reshape(local_tokens, item_total, head_width),...  13.7 us
    slice x9, local copies, waits for them, and re-layouts, body(): padded[:, row_shift:row_shift + PATCH, col_shift:col_shift + pix_cols, :]  11.6 us
    all_to_all x1, starting transfers between devices, body(): lax.all_to_all(stacked, 'seq', split_axis=0, concat_axis=1, tiled=True)  9.88 us
  transfers between devices with their start and end apart: 6, of which 5 were waited for; matrix products, arithmetic and copies ran while one was open for 2% of the time, Pallas kernels for 0%

profile of v1, /device:TPU:1, one launch (start us, length us, event | category | flops | bytes accessed | tf_op | source)
XLA Modules:
  0.0 198.1 jit_solution(9239510435881360642)
XLA Ops:
  0.7 1.5 reshape.139
  2.1 1.0 copy.71
  3.1 13.7 %all-to-all-start = ((bf16[64,32,128]{2,0,1:T(8,128)(2,1)}), bf16[64,32,128]{2,0,1:T(8,128)(2,1)S(1)}, u32[]{:S(2)}, u32[]{:S(2)}) async-start(bf16[64,32,128]{2,0,1:T(8,128)(2,1)} %copy.71), calls=%async_computation | async-start | bytes 1048576 | tf_op jit(solution)/shard_map/all_to_all | solution.py:194
  16.8 0.3 reshape.140
  17.2 1.0 copy.72
  18.2 14.9 %all-to-all-done = bf16[64,32,128]{2,0,1:T(8,128)(2,1)S(1)} async-done(((bf16[64,32,128]{2,0,1:T(8,128)(2,1)}), bf16[64,32,128]{2,0,1:T(8,128)(2,1)S(1)}, u32[]{:S(2)}, u32[]{:S(2)}) %all-to-all-start) | async-done | bytes 524320 | tf_op jit(solution)/shard_map/all_to_all | solution.py:194
  33.1 5.3 %all-to-all-start.1 = ((bf16[64,32,128]{2,0,1:T(8,128)(2,1)}), bf16[64,32,128]{2,0,1:T(8,128)(2,1)S(1)}, u32[]{:S(2)}, u32[]{:S(2)}) async-start(bf16[64,32,128]{2,0,1:T(8,128)(2,1)} %copy.72), calls=%async_computation.1 | async-start | bytes 1048576 | tf_op jit(solution)/shard_map/all_to_all | solution.py:201
  38.4 0.3 reshape.141
  38.7 1.0 copy.73
  39.7 13.9 %all-to-all-done.1 = bf16[64,32,128]{2,0,1:T(8,128)(2,1)S(1)} async-done(((bf16[64,32,128]{2,0,1:T(8,128)(2,1)}), bf16[64,32,128]{2,0,1:T(8,128)(2,1)S(1)}, u32[]{:S(2)}, u32[]{:S(2)}) %all-to-all-start.1) | async-done | bytes 524320 | tf_op jit(solution)/shard_map/all_to_all | solution.py:201
  53.6 6.3 %all-to-all-start.2 = ((bf16[64,32,128]{2,0,1:T(8,128)(2,1)}), bf16[64,32,128]{2,0,1:T(8,128)(2,1)S(1)}, u32[]{:S(2)}, u32[]{:S(2)}) async-start(bf16[64,32,128]{2,0,1:T(8,128)(2,1)} %copy.73), calls=%async_computation.2 | async-start | bytes 1048576 | tf_op jit(solution)/shard_map/all_to_all | solution.py:208
  59.9 0.7 fusion.66
  61.4 13.8 %all-to-all-done.2 = bf16[64,32,128]{2,0,1:T(8,128)(2,1)S(1)} async-done(((bf16[64,32,128]{2,0,1:T(8,128)(2,1)}), bf16[64,32,128]{2,0,1:T(8,128)(2,1)S(1)}, u32[]{:S(2)}, u32[]{:S(2)}) %all-to-all-start.2) | async-done | bytes 524320 | tf_op jit(solution)/shard_map/all_to_all | solution.py:208
  75.2 10.7 %while.11 = (s32[]{:T(128)}, bf16[2048,128]{1,0:T(8,128)(2,1)S(1)}, s32[]{:T(128)}, bf16[2048,128]{1,0:T(8,128)(2,1)S(1)}, bf16[2048,128]{1,0:T(8,128)(2,1)S(1)}...) while((s32[]{:T(128)}, bf16[2048,128]{1,0:T(8,128)(2,1)S(1)}, ...), condition=%wide.region_4.5_spmd.clone, body=%wide.region_1.4_spmd.clone.sunk | while | flops 548537344 | bytes 13912231 | solution.py:178
  75.2 0.7 iota_compare_fusion.4
  75.9 0.8 fusion.105
  76.8 0.9 fusion.106
  77.7 1.1 fusion.107
  78.8 0.7 iota_compare_fusion.4
  79.5 0.9 fusion.105
  80.4 0.9 fusion.106
  81.3 1.1 fusion.107
  82.4 0.7 iota_compare_fusion.4
  83.1 0.8 fusion.105
  83.9 0.9 fusion.106
  84.9 1.1 fusion.107
  85.9 0.5 broadcast.85
  86.5 1.0 reduce.4
  87.5 0.9 reshape.167
  88.4 9.9 %all-to-all-start.3 = ((bf16[32,2,4096]{2,1,0:T(2,128)(2,1)}), bf16[32,2,4096]{2,1,0:T(2,128)(2,1)S(1)}, u32[]{:S(2)}, u32[]{:S(2)}) async-start(bf16[32,2,4096]{2,1,0:T(2,128)(2,1)} %reshape.167), calls=%async_computation.3 | async-start | bytes 1048576 | tf_op jit(solution)/shard_map/all_to_all | solution.py:221
  98.4 16.0 %all-to-all-done.3 = bf16[32,2,4096]{2,1,0:T(2,128)(2,1)S(1)} async-done(((bf16[32,2,4096]{2,1,0:T(2,128)(2,1)}), bf16[32,2,4096]{2,1,0:T(2,128)(2,1)S(1)}, u32[]{:S(2)}, u32[]{:S(2)}) %all-to-all-start.3) | async-done | bytes 524320 | tf_op jit(solution)/shard_map/all_to_all | solution.py:221
  114.4 0.5 reshape.168
  115.0 1.1 convert_element_type.49
  116.1 0.3 reduce_sum.44
  116.5 0.6 multiply_reduce_fusion
  117.4 0.4 copy.75
  118.1 2.5 %collective-permute-start = (bf16[2,1,256,128]{2,3,1,0:T(8,128)(2,1)S(1)}, bf16[2,1,256,128]{2,3,1,0:T(8,128)(2,1)S(1)}, u32[]{:S(2)}, u32[]{:S(2)}) collective-permute-start(bf16[2,1,256,128]{2,3,1,0:T(8,128)(2,1)S(1)} %get-tuple-element.83), channel_id=1, source_target_pairs={{0,1},{1,2},{2,3},{3,4},{4,5},{5,6},{6,7},{7,8},{8,9},{9,10},{10,1... | collective-permute-start | bytes 393224 | tf_op jit(solution)/shard_map/ppermute | solution.py:146
  120.6 1.5 collective-permute-start.1
  122.1 1.0 copy.90
  123.1 4.0 %collective-permute-done.1 = bf16[2,1,256,128]{2,3,1,0:T(8,128)(2,1)S(1)} collective-permute-done((bf16[2,1,256,128]{2,3,1,0:T(8,128)(2,1)S(1)}, bf16[2,1,256,128]{2,3,1,0:T(8,128)(2,1)S(1)}, u32[]{:S(2)}, u32[]{:S(2)}) %collective-permute-start.1) | collective-permute-done | bytes 131104 | tf_op jit(solution)/shard_map/ppermute | solution.py:147
  127.1 0.6 fusion.28
  127.8 1.8 fusion.75
  129.6 0.9 fusion.37
  130.5 0.9 fusion.30
  131.4 1.0 fusion.36
  132.4 0.9 fusion.35
  133.4 0.9 fusion.34
  134.3 1.0 fusion.33
  135.3 0.9 fusion.32
  136.2 0.9 fusion.29
  137.1 1.0 fusion.31.g_ref
  138.1 43.3 %reduce_all.1 = f32[9,16,8,128]{3,2,1,0:T(8,128)} custom-call(f32[9,16,8,128]{3,2,1,0:T(8,128)} %fusion.31.g_ref), custom_call_target="tpu_custom_call" | custom-call | tf_op jit(solution)/shard_map/reduce_all/pallas_call | solution.py:122
  181.4 1.1 pad_maximum_fusion
  182.5 2.1 %copy.81 = bf16[2,4,256,128]{3,2,1,0:T(8,128)(2,1)} copy(bf16[2,4,256,128]{2,3,1,0:T(8,128)(2,1)} %get-tuple-element.82) | data formatting | bytes 1048576 | tf_op jit(solution)/shard_map/slice | solution.py:244
  184.6 2.0 %copy.79 = bf16[2,4,256,128]{3,2,1,0:T(8,128)(2,1)} copy(bf16[2,4,256,128]{2,3,1,0:T(8,128)(2,1)} %get-tuple-element.80) | data formatting | bytes 1048576 | tf_op jit(solution)/shard_map/slice | solution.py:244
  186.7 2.1 %copy.82 = bf16[2,4,256,128]{3,2,1,0:T(8,128)(2,1)} copy(bf16[2,4,256,128]{2,3,1,0:T(8,128)(2,1)} %get-tuple-element.79) | data formatting | bytes 1048576 | tf_op jit(solution)/shard_map/slice | solution.py:244
  188.7 1.0 copy.83
  189.7 1.0 copy.85
  190.7 1.0 copy.86
  192.6 1.4 convolution_add_fusion.7
  194.3 0.3 convolution_add_fusion.5
  194.9 0.5 copy-done.7
  196.2 1.1 fusion.22
  197.3 0.8 copy.118
  (49 shorter events, 3.0 us)
Async XLA Ops:
  0.6 129.0 %copy-start = (bf16[2,4,256,128]{3,2,1,0:T(8,128)(2,1)S(1)}, bf16[2,4,256,128]{3,2,1,0:T(8,128)(2,1)}, u32[]{:S(2)}) copy-start(bf16[2,4,256,128]{3,2,1,0:T(8,128)(2,1)} %param.15) | copy-start | bytes 1572868
  0.6 16.2 %copy-start.10 = (bf16[64,2,2048]{2,1,0:T(2,128)(2,1)S(1)}, bf16[64,2,2048]{2,1,0:T(2,128)(2,1)}, u32[]{:S(2)}) copy-start(bf16[64,2,2048]{2,1,0:T(2,128)(2,1)} %param.10) | copy-start | bytes 1572868
  2.1 36.3 %copy-start.11 = (bf16[64,2,2048]{2,1,0:T(2,128)(2,1)S(1)}, bf16[64,2,2048]{2,1,0:T(2,128)(2,1)}, u32[]{:S(2)}) copy-start(bf16[64,2,2048]{2,1,0:T(2,128)(2,1)} %param.11) | copy-start | bytes 1572868
  3.1 30.0 %all-to-all-start = ((bf16[64,32,128]{2,0,1:T(8,128)(2,1)}), bf16[64,32,128]{2,0,1:T(8,128)(2,1)S(1)}, u32[]{:S(2)}, u32[]{:S(2)}) async-start(bf16[64,32,128]{2,0,1:T(8,128)(2,1)} %copy.71), calls=%async_computation | async-start | bytes 1048576 | tf_op jit(solution)/shard_map/all_to_all | solution.py:194
  18.2 41.8 %copy-start.14 = (s32[2]{0:T(128)S(1)}, s32[2]{0:T(128)}, u32[]{:S(2)}) copy-start(s32[2]{0:T(128)} %param.12) | copy-start | bytes 28
  33.1 20.5 %all-to-all-start.1 = ((bf16[64,32,128]{2,0,1:T(8,128)(2,1)}), bf16[64,32,128]{2,0,1:T(8,128)(2,1)S(1)}, u32[]{:S(2)}, u32[]{:S(2)}) async-start(bf16[64,32,128]{2,0,1:T(8,128)(2,1)} %copy.72), calls=%async_computation.1 | async-start | bytes 1048576 | tf_op jit(solution)/shard_map/all_to_all | solution.py:201
  53.6 21.5 %all-to-all-start.2 = ((bf16[64,32,128]{2,0,1:T(8,128)(2,1)}), bf16[64,32,128]{2,0,1:T(8,128)(2,1)S(1)}, u32[]{:S(2)}, u32[]{:S(2)}) async-start(bf16[64,32,128]{2,0,1:T(8,128)(2,1)} %copy.73), calls=%async_computation.2 | async-start | bytes 1048576 | tf_op jit(solution)/shard_map/all_to_all | solution.py:208
  88.4 26.0 %all-to-all-start.3 = ((bf16[32,2,4096]{2,1,0:T(2,128)(2,1)}), bf16[32,2,4096]{2,1,0:T(2,128)(2,1)S(1)}, u32[]{:S(2)}, u32[]{:S(2)}) async-start(bf16[32,2,4096]{2,1,0:T(2,128)(2,1)} %reshape.167), calls=%async_computation.3 | async-start | bytes 1048576 | tf_op jit(solution)/shard_map/all_to_all | solution.py:221
  115.0 2.2 %copy-start.13 = (f32[2048]{0:T(1024)S(1)}, f32[2048]{0:T(1024)}, u32[]{:S(2)}) copy-start(f32[2048]{0:T(1024)} %param.13) | copy-start | bytes 24580
  118.1 5.0 %collective-permute-start = (bf16[2,1,256,128]{2,3,1,0:T(8,128)(2,1)S(1)}, bf16[2,1,256,128]{2,3,1,0:T(8,128)(2,1)S(1)}, u32[]{:S(2)}, u32[]{:S(2)}) collective-permute-start(bf16[2,1,256,128]{2,3,1,0:T(8,128)(2,1)S(1)} %get-tuple-element.83), channel_id=1, source_target_pairs={{0,1},{1,2},{2,3},{3,4},{4,5},{5,6},{6,7},{7,8},{8,9},{9,10},{10,1... | collective-permute-start | bytes 393224 | tf_op jit(solution)/shard_map/ppermute | solution.py:146
  120.6 6.5 %collective-permute-start.1 = (bf16[2,1,256,128]{2,3,1,0:T(8,128)(2,1)S(1)}, bf16[2,1,256,128]{2,3,1,0:T(8,128)(2,1)S(1)}, u32[]{:S(2)}, u32[]{:S(2)}) collective-permute-start(bf16[2,1,256,128]{2,3,1,0:T(8,128)(2,1)S(1)} %get-tuple-element.84), channel_id=1, source_target_pairs={{1,0},{2,1},{3,2},{4,3},{5,4},{6,5},{7,6},{8,7},{9,8},{10,9},{11,1... | collective-permute-start | bytes 393224 | tf_op jit(solution)/shard_map/ppermute | solution.py:147
  129.6 3.8 %copy-start.5 = (bf16[128,2,4,256]{3,0,2,1:T(8,128)(2,1)S(1)}, bf16[128,2,4,256]{3,0,2,1:T(8,128)(2,1)}, u32[]{:S(2)}) copy-start(bf16[128,2,4,256]{3,0,2,1:T(8,128)(2,1)} %copy.90) | copy-start | bytes 1572868
  182.5 6.2 %copy-start.2 = (bf16[2,4,256,128]{2,3,1,0:T(8,128)(2,1)S(1)}, bf16[2,4,256,128]{2,3,1,0:T(8,128)(2,1)}, u32[]{:S(2)}) copy-start(bf16[2,4,256,128]{2,3,1,0:T(8,128)(2,1)} %get-tuple-element.78) | copy-start | bytes 1572868
  189.7 2.0 %copy-start.3 = (bf16[2,4,256,128]{2,3,1,0:T(8,128)(2,1)S(1)}, bf16[2,4,256,128]{2,3,1,0:T(8,128)(2,1)}, u32[]{:S(2)}) copy-start(bf16[2,4,256,128]{2,3,1,0:T(8,128)(2,1)} %get-tuple-element.81) | copy-start | bytes 1572868
  189.7 2.6 %copy-start.12 = (bf16[9,128,128]{2,1,0:T(8,128)(2,1)S(1)}, bf16[9,128,128]{2,1,0:T(8,128)(2,1)}, u32[]{:S(2)}) copy-start(bf16[9,128,128]{2,1,0:T(8,128)(2,1)} %param.14) | copy-start | bytes 884740
  190.7 1.6 copy-start.4
  192.3 1.7 copy-start.9
  192.6 1.7 copy-start.8
  194.3 1.0 copy-start.7
  194.6 1.1 copy-start.6
  195.9 1.4 copy-start.1

commit v2 on v1

v2 whole, which is shorter than its diff:
```python
import functools
import math

import jax
import jax.numpy as jnp
from jax import lax
from jax.experimental import pallas as pl
from jax.experimental.pallas import tpu as pltpu
from jax.sharding import PartitionSpec as P

HEADS = 16
PATCH = 4
MESH = pl.DeviceIdType.MESH
X, Z = 4, 8
TOK, HD = 64, 128
OWNED = 18
F32, BF16 = jnp.float32, jnp.bfloat16


def remote(src, dst, send, recv, device):
    return pltpu.make_async_remote_copy(
        src_ref=src, dst_ref=dst, send_sem=send, recv_sem=recv, device_id=device, device_id_type=MESH
    )


def wait_bytes(ref, sem):
    pltpu.make_async_copy(ref, ref, sem).wait()


def step_kernel(n_dp, lens_ref, q_ref, k_ref, v_ref, gain_ref, w_ref, cot_ref, dec_ref, wg_ref,
                stage, rq, rk, rv, hold, probs, sums, o_mid, o_in, o_hold, att, ext, cot_t, grid, wide,
                grads, taps, buf1, acc1, buf2, acc2, buf3, fin,
                sx, rx, sz, rz, rr, so, ro, rro, sx2, rx2, sh, rh,
                s1, r1, s2, r2, s3, r3, s4, r4, s5, r5, s6, r6):
    dp, seq = lax.axis_index("dp"), lax.axis_index("seq")
    n_seq = X * Z
    n_yz = (n_dp // 2) * Z
    core, z, x = dp % 2, seq // X, seq % X
    member = (dp // 2) * Z + z
    partner = (dp + 1 - 2 * core, seq)
    half = 2 + 4 * core

    def x_device(step):
        return (dp, z * X + (x + step) % X)

    def z_device(step):
        return (dp, ((z + step) % Z) * X + x)

    def yz_device(index):
        return ((index // Z) * 2 + core, (index % Z) * X + x)

    barrier = pltpu.get_barrier_semaphore()

    def signal(device):
        pl.semaphore_signal(barrier, inc=1, device_id=device, device_id_type=MESH)

    def greet(step, _):
        signal(yz_device((member + step) % n_yz))
        return 0

    for step in range(1, X):
        signal(x_device(step))
    lax.fori_loop(1, n_yz, greet, 0)
    signal(partner)
    signal((dp, (seq + 1) % n_seq))
    signal((dp, (seq + n_seq - 1) % n_seq))
    pl.semaphore_wait(barrier, (X - 1) + (n_yz - 1) + 1 + 2)

    sources, landed = (q_ref, k_ref, v_ref), (rq, rk, rv)
    far_first = (4, 3, 5, 2, 6, 1, 7)

    x_copies = []
    for array in range(3):
        for step in (1, 3, 2):
            copy = remote(sources[array].at[:, (x + step) % X], stage.at[array, :, x],
                          sx.at[array, step - 1], rx.at[array, step - 1], x_device(step))
            copy.start()
            x_copies.append(copy)

    def along_z(array, blocks, column):
        for step in far_first:
            block = blocks.at[(z + step) % Z, column]
            if step == 4:
                remote(block, hold.at[array, column], sz.at[array], rr.at[array, column], z_device(half)).start()
            else:
                remote(block, landed[array].at[z, column], sz.at[array], rz.at[array], z_device(step)).start()

    def staged(array):
        for step in (1, 3, 2):
            column = (x + X - step) % X
            wait_bytes(stage.at[array, :, column], rx.at[array, step - 1])
            along_z(array, stage.at[array], column)
            landed[array][z, column] = stage[array, z, column]
        landed[array][z, x] = sources[array][z, x]

    def onward(array, column):
        wait_bytes(hold.at[array, column], rr.at[array, column])
        remote(hold.at[array, column], landed[array].at[(z + Z - half) % Z, column], sz.at[array], rz.at[array],
               z_device(half)).start()

    for array in range(3):
        along_z(array, sources[array], x)

    for row in range(PATCH):
        for region in range(2):
            grid[region] = cot_ref[region, row].astype(F32)
        for px in range(PATCH):
            part = [grid[region, pl.ds(px, TOK, stride=PATCH), :] for region in range(2)]
            cot_t[px * HD:(px + 1) * HD, row * 2 * TOK:(row + 1) * 2 * TOK] = jnp.concatenate(part).T.astype(BF16)
    wide[...] = jnp.zeros_like(wide)
    for dy in range(3):
        for dx in range(3):
            for px in range(PATCH):
                wide[dy, (px + dx) * HD:(px + dx + 1) * HD, px * HD:(px + 1) * HD] = w_ref[3 * dy + dx]

    columns = [x] + [(x + X - step) % X for step in (1, 3, 2)]
    staged(0)
    staged(1)
    for column in columns:
        onward(0, column)
    staged(2)
    for column in columns:
        onward(1, column)

    region_len = lens_ref[seq // HEADS]
    key_slot = lax.broadcasted_iota(jnp.int32, (1, n_seq * TOK), 1)
    bias = jnp.where(key_slot < region_len, 0.0, -1e30).astype(F32)
    factor = math.log2(math.e) / math.sqrt(HD)
    for array in range(2):
        wait_bytes(landed[array].at[pl.ds(0, Z - 1)], rz.at[array])

    def powers(index, _):
        query = rq[index].reshape(X * TOK, HD)
        keys = rk[...].reshape(n_seq * TOK, HD)
        scores = lax.dot_general(query, keys, (((1,), (1,)), ((), ())), preferred_element_type=F32) + bias
        top = jnp.max(scores, axis=1, keepdims=True)
        power = jnp.exp2((scores - top) * factor)
        sums[index] = jnp.sum(power, axis=1, keepdims=True)
        probs[index] = power.astype(BF16)
        return 0

    for quarter in range(4):
        lax.fori_loop(2 * quarter, 2 * quarter + 2, powers, 0)
        onward(2, columns[quarter])
    wait_bytes(rv.at[pl.ds(0, Z - 1)], rz.at[2])

    def mixed(step):
        to = (z + step) % Z
        out = jnp.dot(probs[to], rv[...].reshape(n_seq * TOK, HD), preferred_element_type=F32) / sums[to]
        o_mid[to] = out.astype(BF16).reshape(X, TOK, HD)
        return o_mid.at[to]

    for step in far_first:
        block = mixed(step)
        if step == 4:
            remote(block, o_hold, so, rro, z_device(half)).start()
        else:
            remote(block, o_in.at[z], so, ro.at[step - 1], z_device(step)).start()
    own = mixed(0)

    def along_x(blocks, index):
        for step in (2, 1, 3):
            remote(blocks.at[index, (x + step) % X], att.at[index, x], sx2, rx2.at[step - 1], x_device(step)).start()
        att[index, x] = blocks[index, x]

    wait_bytes(o_hold, rro)
    remote(o_hold, o_in.at[(z + Z - half) % Z], so, ro.at[3], z_device(half)).start()
    along_x(o_mid, z)
    for step in (1, 7, 2, 6, 3, 5, 4):
        index = (z + Z - step) % Z
        wait_bytes(o_in.at[index], ro.at[step - 1])
        along_x(o_in, index)
    for step in range(1, X):
        wait_bytes(att.at[pl.ds(0, 2)], rx2.at[step - 1])

    row_of = lax.broadcasted_iota(jnp.int32, (TOK, HD), 0)

    def put_sides(row, region, first, last):
        rows = pl.ds(region * TOK, TOK)
        before = jnp.where(row_of == 0, 0.0, pltpu.roll(last, 1, 0))
        after = jnp.where(row_of == TOK - 1, 0.0, pltpu.roll(first, TOK - 1, 0))
        ext[row, rows, 0:HD] = before.astype(BF16)
        ext[row, rows, 5 * HD:6 * HD] = after.astype(BF16)

    for region in range(2):
        values = att[4 * region:4 * region + 4].astype(F32)
        count = 1.0 / (HEADS * HD)
        mean = jnp.sum(jnp.sum(values, axis=(0, 1)), axis=1, keepdims=True) * count
        centered = values - mean
        var = jnp.sum(jnp.sum(centered * centered, axis=(0, 1)), axis=1, keepdims=True) * count
        scale = lax.rsqrt(var + 1e-05)
        live = seq * TOK + row_of < lens_ref[region]
        for py in range(PATCH):
            line = []
            for px in range(PATCH):
                head = PATCH * py + px
                normed = centered[py, px] * scale * gain_ref[head:head + 1, :]
                normed = jnp.where(live, normed, 0.0)
                ext[py + 1, region * TOK:(region + 1) * TOK, (px + 1) * HD:(px + 2) * HD] = normed.astype(BF16)
                line.append(normed)
            put_sides(py + 1, region, line[0], line[3])

    middle = pl.ds(HD, PATCH * HD)
    down = remote(ext.at[4, :, middle], ext.at[0, :, middle], sh.at[0], rh.at[0], (dp, (seq + 1) % n_seq))
    up = remote(ext.at[1, :, middle], ext.at[5, :, middle], sh.at[1], rh.at[1], (dp, (seq + n_seq - 1) % n_seq))

    @pl.when(seq < n_seq - 1)
    def _():
        down.start()

    @pl.when(seq > 0)
    def _():
        up.start()

    def lines(low, high):
        return ext[low:high].reshape((high - low) * 2 * TOK, 6 * HD)

    def turned(low, high):
        return cot_t[:, low * 2 * TOK:high * 2 * TOK]

    def grad_of(low, high, first):
        return jnp.dot(turned(low, high), lines(first, first + high - low), preferred_element_type=F32)

    grads[1] = grad_of(0, 4, 1)
    grads[0] = grad_of(1, 4, 1)
    grads[2] = grad_of(0, 3, 2)

    @pl.when(seq < n_seq - 1)
    def _():
        down.wait_send()
        wait_bytes(ext.at[5, :, middle], rh.at[1])

    @pl.when(seq > 0)
    def _():
        up.wait_send()
        wait_bytes(ext.at[0, :, middle], rh.at[0])

    @pl.when(seq == 0)
    def _():
        ext[0] = jnp.zeros((2 * TOK, 6 * HD), BF16)

    @pl.when(seq == n_seq - 1)
    def _():
        ext[5] = jnp.zeros((2 * TOK, 6 * HD), BF16)

    for row in (0, 5):
        for region in range(2):
            rows = pl.ds(region * TOK, TOK)
            put_sides(row, region, ext[row, rows, HD:2 * HD].astype(F32), ext[row, rows, 4 * HD:5 * HD].astype(F32))
    grads[0] += grad_of(0, 1, 0)
    grads[2] += grad_of(3, 4, 5)
    for dy in range(3):
        for dx in range(3):
            total = grads[dy, 0:HD, dx * HD:(dx + 1) * HD]
            for px in range(1, PATCH):
                total += grads[dy, px * HD:(px + 1) * HD, (px + dx) * HD:(px + dx + 1) * HD]
            taps[3 * dy + dx] = total.T.reshape(16, 8, HD)

    swap = remote(taps.at[:, pl.ds(8 * (1 - core), 8)], buf1, s1, r1, partner)
    swap.start()
    swap.wait()
    acc1[...] = taps[:, pl.ds(8 * core, 8)] + buf1[...]
    copies = []
    for step in range(1, X):
        to = (x + step) % X
        copy = remote(acc1.at[:, pl.ds(2 * to, 2)], buf2.at[step - 1], s2.at[step - 1], r2.at[step - 1],
                      x_device(step))
        copy.start()
        copies.append(copy)
    for copy in copies:
        copy.wait()
    acc2[...] = (acc1[:, pl.ds(2 * x, 2)] + buf2[0]) + (buf2[1] + buf2[2])
    offset = (member + n_yz - core) % n_yz
    for tile in range(OWNED):
        owner = (3 * tile + core) % n_yz

        @pl.when(owner != member)
        def _():
            remote(acc2.at[tile // 2, tile % 2], buf3.at[member], s3, r3, yz_device(owner)).start()

    decoded = jnp.dot(lines(0, 4), wide[0], preferred_element_type=F32)
    decoded += jnp.dot(lines(1, 5), wide[1], preferred_element_type=F32)
    decoded += jnp.dot(lines(2, 6), wide[2], preferred_element_type=F32)
    for row in range(PATCH):
        for region in range(2):
            low = (row * 2 + region) * TOK
            for px in range(PATCH):
                grid[region, pl.ds(px, TOK, stride=PATCH), :] = decoded[low:low + TOK, px * HD:(px + 1) * HD]
            dec_ref[region, row] = grid[region].astype(BF16)

    mine = offset // 3
    owns = jnp.logical_and(offset % 3 == 0, mine < OWNED)

    @pl.when(owns)
    def _():
        wait_bytes(buf3.at[pl.ds(0, OWNED - 1)], s3)
        wait_bytes(buf3.at[pl.ds(0, n_yz - 1)], r3)
        buf3[member] = acc2[mine // 2, mine % 2]
        fin[mine // 2, mine % 2] = jnp.sum(buf3[...], axis=0) * (1.0 / math.sqrt(PATCH * PATCH * TOK))
        part = fin.at[mine // 2, mine % 2]

        def spread(step, _):
            remote(part, part, s4, r4, yz_device((member + step) % n_yz)).start()
            return 0

        lax.fori_loop(1, n_yz, spread, 0)
        wait_bytes(buf3.at[pl.ds(0, n_yz - 1)], s4)
        wait_bytes(buf3.at[pl.ds(0, OWNED - 1)], r4)

    @pl.when(jnp.logical_not(owns))
    def _():
        wait_bytes(buf3.at[pl.ds(0, OWNED)], s3)
        wait_bytes(buf3.at[pl.ds(0, OWNED)], r4)

    def place(which):
        return wg_ref.at[:, pl.ds(8 * core + 2 * which, 2)]

    copies = []
    for step in range(1, X):
        copy = remote(fin, place(x), s5.at[step - 1], r5.at[step - 1], x_device(step))
        copy.start()
        copies.append(copy)
    wg_ref[:, pl.ds(8 * core + 2 * x, 2)] = fin[...]
    forwards = [remote(fin, place(x), s6.at[0], r6.at[0], partner)]
    forwards[0].start()
    for step in range(1, X):
        copies[step - 1].wait()
        came = place((x + X - step) % X)
        forward = remote(came, came, s6.at[step], r6.at[step], partner)
        forward.start()
        forwards.append(forward)

    for copy in x_copies:
        copy.wait_send()
    for array in range(3):
        wait_bytes(landed[array], sz.at[array])
    wait_bytes(o_in, so)
    wait_bytes(att.at[pl.ds(0, 6)], sx2)
    for forward in forwards:
        forward.wait()


def body(query_rows, key_rows, value_rows, region_lengths, norm_gain, conv_weight, cotangent):
    n_dp = lax.axis_size("dp")
    n_yz = (n_dp // 2) * Z

    def items(rows):
        return rows.reshape(TOK, X * Z, HD).transpose(1, 0, 2).reshape(Z, X, TOK, HD)

    vmem = pl.BlockSpec(memory_space=pltpu.VMEM)
    dma = pltpu.SemaphoreType.DMA
    decoded, grad = pl.pallas_call(
        functools.partial(step_kernel, n_dp),
        out_shape=(jax.ShapeDtypeStruct((2, 4, 256, 128), BF16), jax.ShapeDtypeStruct((9, 16, 8, 128), F32)),
        in_specs=[pl.BlockSpec(memory_space=pltpu.SMEM)] + [vmem] * 6,
        out_specs=(vmem, vmem),
        scratch_shapes=[
            pltpu.VMEM((3, Z, X, TOK, HD), BF16),
            pltpu.VMEM((Z, X, TOK, HD), BF16),
            pltpu.VMEM((Z, X, TOK, HD), BF16),
            pltpu.VMEM((Z, X, TOK, HD), BF16),
            pltpu.VMEM((3, X, TOK, HD), BF16),
            pltpu.VMEM((Z, X * TOK, X * Z * TOK), BF16),
            pltpu.VMEM((Z, X * TOK, 1), F32),
            pltpu.VMEM((Z, X, TOK, HD), BF16),
            pltpu.VMEM((Z, X, TOK, HD), BF16),
            pltpu.VMEM((X, TOK, HD), BF16),
            pltpu.VMEM((Z, X, TOK, HD), BF16),
            pltpu.VMEM((6, 2 * TOK, 6 * HD), BF16),
            pltpu.VMEM((4 * HD, 8 * TOK), BF16),
            pltpu.VMEM((2, PATCH * TOK, HD), F32),
            pltpu.VMEM((3, 6 * HD, 4 * HD), BF16),
            pltpu.VMEM((3, 4 * HD, 6 * HD), F32),
            pltpu.VMEM((9, 16, 8, HD), F32),
            pltpu.VMEM((9, 8, 8, HD), F32),
            pltpu.VMEM((9, 8, 8, HD), F32),
            pltpu.VMEM((3, 9, 2, 8, HD), F32),
            pltpu.VMEM((9, 2, 8, HD), F32),
            pltpu.VMEM((n_yz, 8, HD), F32),
            pltpu.VMEM((9, 2, 8, HD), F32),
            dma((3, 3)), dma((3, 3)), dma((3,)), dma((3,)), dma((3, X)),
            dma, dma((7,)), dma, dma, dma((3,)), dma((2,)), dma((2,)),
            dma, dma, dma((3,)), dma((3,)), dma, dma, dma, dma, dma((3,)), dma((3,)), dma((4,)), dma((4,)),
        ],
        compiler_params=pltpu.CompilerParams(
            collective_id=0, has_side_effects=True, vmem_limit_bytes=60 * 1024 * 1024
        ),
        name="region_step",
    )(
        region_lengths,
        items(query_rows),
        items(key_rows),
        items(value_rows),
        norm_gain.reshape(HEADS, HD),
        conv_weight,
        cotangent,
    )
    return decoded, grad.reshape(9, 128, 128)


def solution(mesh):
    placed = (
        P("seq", "dp", None),
        P("seq", "dp", None),
        P("seq", "dp", None),
        P("dp"),
        P(),
        P(),
        P("dp", "seq", None, None),
    )
    return jax.shard_map(
        body,
        mesh=mesh,
        in_specs=placed,
        out_specs=(P("dp", "seq", None, None), P()),
        check_vma=False,
    )
```

time: 200 us -> 129 us (0.65)
  Pallas kernels: 43.3 us -> 120 us
  waiting for transfers between devices: 62.6 us -> 0 us
  starting transfers between devices: 39.1 us -> 0 us
  matrix products: 18.6 us -> 0 us
  local copies, waits for them, and re-layouts: 21.8 us -> 7.86 us
  other arithmetic: 10.9 us -> 0 us
    pallas_call x1, Pallas kernels: 43.3 us -> 120 us  [body(): pl.pallas_call(functools.partial(step_kernel, n_dp), out_shape=(jax.Shape...]
    all_to_all x4 -> x0, waiting for transfers between devices: 58.6 us -> none  [the longest x1 16 us: body(): lax.all_to_all(stacked, 'seq', split_axis=0, concat_axis=1, tiled=True)]
    all_to_all x4 -> x0, starting transfers between devices: 35.1 us -> none  [the longest x1 13.7 us: body(): lax.all_to_all(query_rows.reshape(local_tokens, item_total, head_width),...]
    dot_general x24 -> x0, matrix products: 18.6 us -> none  [the longest x9 8.52 us: body(): jnp.dot(window.T, cot_flat, preferred_element_type=jnp.float32)]
    slice x10 -> x0, local copies, waits for them, and re-layouts: 11.6 us -> none  [the longest x9 11.6 us: body(): padded[:, row_shift:row_shift + PATCH, col_shift:col_shift + pix_cols, :]]
    reduce_sum x8 -> x0, other arithmetic: 4.58 us -> none  [the longest x3 2.84 us: one_block(): totals = jnp.sum(powers, axis=1, keepdims=True)]
    ppermute x2 -> x0, waiting for transfers between devices: 4 us -> none  [the longest x1 4 us: extended(): after = lax.ppermute(initial, axis, down)]
    ppermute x2 -> x0, starting transfers between devices: 3.99 us -> none  [the longest x1 2.51 us: extended(): before = lax.ppermute(last, axis, up)]
  transfers between devices with their start and end apart: 6 -> 0, of which waited for: 5 -> 0; matrix products, arithmetic and copies ran while one was open for 2% -> 0% of each run, Pallas kernels for 0% -> 0%
where the time goes in v2:
time: 129 us; the launch traced here: 128 us
  Pallas kernels  120 us (93%)
  local copies, waits for them, and re-layouts  7.86 us (6%)
    pallas_call x1, Pallas kernels, body(): pl.pallas_call(functools.partial(step_kernel, n_dp), out_shape=(jax.Shape...  120 us
    reshape x6, local copies, waits for them, and re-layouts, items(): rows.reshape(TOK, X * Z, HD).transpose(1, 0, 2).reshape(Z, X, TOK, HD)  5.03 us
    unnamed x8, local copies, waits for them, and re-layouts  2.83 us

profile of v2, /device:TPU:1, one launch (start us, length us, event | category | flops | bytes accessed | tf_op | source)
XLA Modules:
  0.0 128.4 jit_solution(13077344840336980636)
XLA Ops:
  0.6 1.4 %reshape.28 = bf16[64,32,128]{2,1,0:T(8,128)(2,1)S(1)} reshape(bf16[64,2,2048]{2,1,0:T(2,128)(2,1)} %param.7) | data formatting | bytes 1048576 | tf_op jit(solution)/shard_map/reshape | solution.py:348
  2.0 0.0 copy-start.1
  2.0 1.0 copy.9
  3.0 0.0 copy-done.1
  3.1 0.3 reshape.30
  3.4 0.0 copy-start.2
  3.4 1.0 copy.10
  4.4 0.0 copy-done.2
  4.4 0.3 reshape.32
  4.8 1.0 copy.11
  5.8 119.9 %region_step.1 = (bf16[2,4,256,128]{3,2,1,0:T(8,128)(2,1)}, f32[9,16,8,128]{3,2,1,0:T(8,128)}) custom-call(s32[2]{0:T(128)} %lens_ref.1, bf16[8,4,64,128]{3,2,1,0:T(8,128)(2,1)} %bitcast.11, bf16[8,4,64,128]{3,2,1,0:T(8,128)(2,1)} %bitcast.12, bf16[8,4,64,128]{3,2,1,0:T(8,128)(2,1)} %bitcast.13, f32[16,128]{1,0:T(8,128)} %bitcast.15, ...), custom_call_target="tpu_custom_call" | custom-call | tf_op jit(solution)/shard_map/region_step/pallas_call | solution.py:352
  125.6 0.0 copy-start
  125.6 1.9 %copy.14 = bf16[2,4,256,128]{3,2,1,0:T(8,128)(2,1)} copy(bf16[2,4,256,128]{3,2,1,0:T(8,128)(2,1)} %get-tuple-element.8) | data formatting | bytes 1048576
  127.6 0.0 copy-done
  127.6 0.8 copy.15
Async XLA Ops:
  2.0 1.0 copy-start.1
  3.4 1.0 copy-start.2
  125.6 1.9 %copy-start = (f32[9,16,8,128]{3,2,1,0:T(8,128)S(1)}, f32[9,16,8,128]{3,2,1,0:T(8,128)}, u32[]{:S(2)}) copy-start(f32[9,16,8,128]{3,2,1,0:T(8,128)} %get-tuple-element.5) | copy-start | bytes 1769476

commit v3 on v2

v3 whole, which is shorter than its diff:
```python
import functools
import math

import jax
import jax.numpy as jnp
from jax import lax
from jax.experimental import pallas as pl
from jax.experimental.pallas import tpu as pltpu
from jax.sharding import PartitionSpec as P

HEADS = 16
PATCH = 4
MESH = pl.DeviceIdType.MESH
X, Z = 4, 8
TOK, HD = 64, 128
OWNED = 18
F32, BF16 = jnp.float32, jnp.bfloat16


def remote(src, dst, send, recv, device):
    return pltpu.make_async_remote_copy(
        src_ref=src, dst_ref=dst, send_sem=send, recv_sem=recv, device_id=device, device_id_type=MESH
    )


def wait_bytes(ref, sem):
    pltpu.make_async_copy(ref, ref, sem).wait()


def step_kernel(n_dp, lens_ref, q_hbm, k_hbm, v_hbm, gain_ref, w_hbm, cot_hbm, dec_ref, wg_ref,
                raw, w_ref, cot_ref, cot_side, pairs, split, stage, rk, rq, rv, hold, probs, sums, o_mid, o_in, o_hold, att, ext, cot_t, grid, wide,
                taps, buf1, acc1, buf2, acc2, buf3, buf4, fin, whole,
                load, sx, rx, sz, rz, rzq, rr, so, ro, rro, sx2, rx2, sh, rh, sc, rc,
                s1, r1, s2, r2, s3, r3, s4, r4, s5, r5, s6, r6):
    dp, seq = lax.axis_index("dp"), lax.axis_index("seq")
    n_seq = X * Z
    n_yz = (n_dp // 2) * Z
    core, z, x = dp % 2, seq // X, seq % X
    member = (dp // 2) * Z + z
    partner = (dp + 1 - 2 * core, seq)
    half = 2 + 4 * core

    def x_device(step):
        return (dp, z * X + (x + step) % X)

    def z_device(step):
        return (dp, ((z + step) % Z) * X + x)

    def yz_device(index):
        return ((index // Z) * 2 + core, (index % Z) * X + x)

    loads = [pltpu.make_async_copy(src, dst, load.at[i]) for i, (src, dst) in enumerate((
        (k_hbm, raw.at[0]), (q_hbm, raw.at[1]), (v_hbm, raw.at[2]), (cot_hbm, cot_ref), (w_hbm, w_ref)))]
    for copy in loads:
        copy.start()

    barrier = pltpu.get_barrier_semaphore()

    def signal(device):
        pl.semaphore_signal(barrier, inc=1, device_id=device, device_id_type=MESH)

    def greet(step, _):
        signal(yz_device((member + step) % n_yz))
        return 0

    for step in range(1, X):
        signal(x_device(step))
    lax.fori_loop(1, n_yz, greet, 0)
    signal(partner)
    signal((dp, (seq + 1) % n_seq))
    signal((dp, (seq + n_seq - 1) % n_seq))

    for array in range(3):
        loads[array].wait()
        for head in range(HEADS):
            both = raw[array, :, :, head * HD:(head + 1) * HD].astype(F32)
            pairs[head % 4] = both.reshape(2 * TOK, HD)
            for region in range(2):
                item = region * HEADS + head
                split[array, item // X, item % X] = pairs[head % 4, pl.ds(region, TOK, stride=2), :].astype(BF16)
    pl.semaphore_wait(barrier, (X - 1) + (n_yz - 1) + 1 + 2)

    landed = (rk, rq, rv)
    far_first = (4, 3, 5, 2, 6, 1, 7)

    x_copies = []
    for array in range(3):
        for step in (1, 3, 2):
            copy = remote(split.at[array, :, (x + step) % X], stage.at[array, :, x],
                          sx.at[array, step - 1], rx.at[array, step - 1], x_device(step))
            copy.start()
            x_copies.append(copy)

    def arrival(array, step):
        return (rz.at[0], rzq.at[step - 1], rz.at[1])[array]

    def along_z(array, blocks, column, step):
        block = blocks.at[(z + step) % Z, column]
        if step == 4:
            remote(block, hold.at[array, column], sz.at[array], rr.at[array, column], z_device(half)).start()
        else:
            remote(block, landed[array].at[z, column], sz.at[array], arrival(array, step), z_device(step)).start()

    others = [(x + X - step) % X for step in (1, 3, 2)]

    def came(array, number):
        wait_bytes(stage.at[array, :, others[number]], rx.at[array, (1, 3, 2)[number] - 1])
        landed[array][z, others[number]] = stage[array, z, others[number]]

    def onward(array, column):
        wait_bytes(hold.at[array, column], rr.at[array, column])
        remote(hold.at[array, column], landed[array].at[(z + Z - half) % Z, column], sz.at[array], arrival(array, 4),
               z_device(half)).start()

    for array in range(3):
        for step in far_first:
            along_z(array, split.at[array], x, step)
        landed[array][z, x] = split[array, z, x]

    loads[3].wait()
    loads[4].wait()

    def turn(row, first, second):
        grid[0], grid[1] = first.astype(F32), second.astype(F32)
        low = (row + 1) * 2 * TOK
        for px in range(PATCH):
            part = [grid[region, pl.ds(px, TOK, stride=PATCH), :] for region in range(2)]
            cot_t[px * HD:(px + 1) * HD, low:low + 2 * TOK] = jnp.concatenate(part).T.astype(BF16)

    for row in range(PATCH):
        turn(row, cot_ref[0, row], cot_ref[1, row])
    wide[...] = jnp.zeros_like(wide)
    for dy in range(3):
        for dx in range(3):
            for px in range(PATCH):
                wide[dy, (px + dx) * HD:(px + dx + 1) * HD, px * HD:(px + 1) * HD] = w_ref[3 * dy + dx]

    columns = [x] + others
    for number in range(3):
        came(0, number)
        for step in far_first:
            along_z(0, stage.at[0], others[number], step)
    for number in range(3):
        came(1, number)
    for step in far_first:
        for column in others:
            along_z(1, stage.at[1], column, step)
    for column in columns:
        onward(0, column)

    region_len = lens_ref[seq // HEADS]
    key_slot = lax.broadcasted_iota(jnp.int32, (1, n_seq * TOK), 1)
    bias = jnp.where(key_slot < region_len, 0.0, -1e30).astype(F32)
    factor = math.log2(math.e) / math.sqrt(HD)

    def powers(step):
        index = (z + Z - step) % Z
        if step:
            wait_bytes(rq.at[index], rzq.at[step - 1])
        query = rq[index].reshape(X * TOK, HD)
        keys = rk[...].reshape(n_seq * TOK, HD)
        scores = lax.dot_general(query, keys, (((1,), (1,)), ((), ())), preferred_element_type=F32) + bias
        top = jnp.max(scores, axis=1, keepdims=True)
        power = jnp.exp2((scores - top) * factor)
        sums[index] = jnp.sum(power, axis=1, keepdims=True)
        probs[index] = power.astype(BF16)

    wait_bytes(rk.at[pl.ds(0, Z - 1)], rz.at[0])
    powers(0)
    for number in range(3):
        came(2, number)
        for step in far_first:
            along_z(2, stage.at[2], others[number], step)
    for column in columns:
        onward(1, column)

    cot_down = remote(cot_ref.at[:, 3], cot_side.at[0], sc.at[0], rc.at[0], (dp, (seq + 1) % n_seq))
    cot_up = remote(cot_ref.at[:, 0], cot_side.at[1], sc.at[1], rc.at[1], (dp, (seq + n_seq - 1) % n_seq))

    @pl.when(x < X - 1)
    def _():
        cot_down.start()

    @pl.when(x > 0)
    def _():
        cot_up.start()

    powers(3)
    powers(5)
    powers(2)
    for column, step in zip(columns, (6, 1, 7)):
        powers(step)
        onward(2, column)
    onward(2, columns[3])
    powers(4)
    wait_bytes(rv.at[pl.ds(0, Z - 1)], rz.at[1])

    def mixed(step):
        to = (z + step) % Z
        out = jnp.dot(probs[to], rv[...].reshape(n_seq * TOK, HD), preferred_element_type=F32) / sums[to]
        o_mid[to] = out.astype(BF16).reshape(X, TOK, HD)

    def home(blocks, column, step):
        block = blocks.at[(z + step) % Z, column]
        if step == 4:
            remote(block, o_hold.at[column], so, rro.at[column], z_device(half)).start()
        else:
            remote(block, att.at[z, column], so, ro, z_device(step)).start()

    for step in far_first + (0,):
        mixed(step)
        to = (z + step) % Z
        for side in (2, 1, 3):
            block = o_mid.at[to, (x + side) % X]
            if step:
                remote(block, o_in.at[to, x], sx2, rx2.at[step - 1, side - 1], x_device(side)).start()
            else:
                remote(block, att.at[z, x], sx2, rx2.at[7, side - 1], x_device(side)).start()
        if step:
            home(o_mid, x, step)
    att[z, x] = o_mid[z, x]

    @pl.when(jnp.logical_and(x == X - 1, seq < n_seq - 1))
    def _():
        cot_down.start()

    @pl.when(jnp.logical_and(x == 0, seq > 0))
    def _():
        cot_up.start()

    def passing(step):
        for side in (1, 3, 2):
            column = (x + X - side) % X
            wait_bytes(o_in.at[(z + step) % Z, column], rx2.at[step - 1, side - 1])
            home(o_in, column, step)

    for step in (4, 3, 5, 2, 6):
        passing(step)
    for column in columns:
        wait_bytes(o_hold.at[column], rro.at[column])
        remote(o_hold.at[column], att.at[(z + Z - half) % Z, column], so, ro, z_device(half)).start()
    for step in (1, 7):
        passing(step)
    for side in range(1, X):
        wait_bytes(att.at[z, (x + X - side) % X], rx2.at[7, side - 1])
    wait_bytes(att.at[pl.ds(0, Z - 1)], ro)

    row_of = lax.broadcasted_iota(jnp.int32, (TOK, HD), 0)

    def put_sides(row, region, first, last):
        rows = pl.ds(region * TOK, TOK)
        before = jnp.where(row_of == 0, 0.0, pltpu.roll(last, 1, 0))
        after = jnp.where(row_of == TOK - 1, 0.0, pltpu.roll(first, TOK - 1, 0))
        ext[row, rows, 0:HD] = before.astype(BF16)
        ext[row, rows, 5 * HD:6 * HD] = after.astype(BF16)

    for region in range(2):
        values = att[4 * region:4 * region + 4].astype(F32)
        count = 1.0 / (HEADS * HD)
        mean = jnp.sum(jnp.sum(values, axis=(0, 1)), axis=1, keepdims=True) * count
        centered = values - mean
        var = jnp.sum(jnp.sum(centered * centered, axis=(0, 1)), axis=1, keepdims=True) * count
        scale = lax.rsqrt(var + 1e-05)
        live = seq * TOK + row_of < lens_ref[region]
        for py in range(PATCH):
            line = []
            for px in range(PATCH):
                head = PATCH * py + px
                normed = centered[py, px] * scale * gain_ref[head:head + 1, :]
                normed = jnp.where(live, normed, 0.0)
                ext[py + 1, region * TOK:(region + 1) * TOK, (px + 1) * HD:(px + 2) * HD] = normed.astype(BF16)
                line.append(normed)
            put_sides(py + 1, region, line[0], line[3])

    middle = pl.ds(HD, PATCH * HD)
    down = remote(ext.at[4, :, middle], ext.at[0, :, middle], sh.at[0], rh.at[0], (dp, (seq + 1) % n_seq))
    up = remote(ext.at[1, :, middle], ext.at[5, :, middle], sh.at[1], rh.at[1], (dp, (seq + n_seq - 1) % n_seq))

    @pl.when(seq < n_seq - 1)
    def _():
        down.start()

    @pl.when(seq > 0)
    def _():
        up.start()

    def lines(low, high):
        return ext[low:high].reshape((high - low) * 2 * TOK, 6 * HD)

    def taps_of(dy):
        low = (2 - dy) * 2 * TOK
        block = jnp.dot(cot_t[:, low:low + PATCH * 2 * TOK], lines(1, 5), preferred_element_type=F32)
        for dx in range(3):
            total = block[0:HD, dx * HD:(dx + 1) * HD]
            for px in range(1, PATCH):
                total += block[px * HD:(px + 1) * HD, (px + dx) * HD:(px + dx + 1) * HD]
            taps[3 * dy + dx] = total.T.reshape(16, 8, HD)

    def three(ref, dy, *rest):
        return ref.at[(pl.ds(3 * dy, 3),) + rest]

    def to_core(dy):
        return remote(three(taps, dy, pl.ds(8 * (1 - core), 8)), three(buf1, dy), s1.at[dy], r1.at[dy], partner)

    def to_x(dy, step):
        return remote(three(acc1, dy, pl.ds(2 * ((x + step) % X), 2)), buf2.at[step - 1, pl.ds(3 * dy, 3)],
                      s2.at[dy, step - 1], r2.at[dy, step - 1], x_device(step))

    def cores_done(dy):
        to_core(dy).wait()
        some = slice(3 * dy, 3 * dy + 3)
        acc1[some] = taps[some, pl.ds(8 * core, 8)] + buf1[some]
        for step in (2, 1, 3):
            to_x(dy, step).start()

    taps_of(1)
    to_core(1).start()

    @pl.when(seq < n_seq - 1)
    def _():
        cot_down.wait_send()
        wait_bytes(cot_side.at[1], rc.at[1])

    @pl.when(seq > 0)
    def _():
        cot_up.wait_send()
        wait_bytes(cot_side.at[0], rc.at[0])

    @pl.when(seq == 0)
    def _():
        cot_side[0] = jnp.zeros((2, PATCH * TOK, HD), BF16)

    @pl.when(seq == n_seq - 1)
    def _():
        cot_side[1] = jnp.zeros((2, PATCH * TOK, HD), BF16)

    turn(PATCH, cot_side[1, 0], cot_side[1, 1])
    taps_of(0)
    to_core(0).start()
    cores_done(1)
    turn(-1, cot_side[0, 0], cot_side[0, 1])
    taps_of(2)
    to_core(2).start()
    cores_done(0)
    cores_done(2)
    for dy in (1, 0, 2):
        for step in range(1, X):
            to_x(dy, step).wait()
        some = slice(3 * dy, 3 * dy + 3)
        acc2[some] = (acc1[some, pl.ds(2 * x, 2)] + buf2[0, some]) + (buf2[1, some] + buf2[2, some])
        for tile in range(6 * dy, 6 * dy + 6):
            owner = (3 * tile + core) % n_yz

            @pl.when(owner != member)
            def _():
                remote(acc2.at[tile // 2, tile % 2], buf3.at[member], s3, r3, yz_device(owner)).start()
    offset = (member + n_yz - core) % n_yz

    @pl.when(seq < n_seq - 1)
    def _():
        down.wait_send()
        wait_bytes(ext.at[5, :, middle], rh.at[1])

    @pl.when(seq > 0)
    def _():
        up.wait_send()
        wait_bytes(ext.at[0, :, middle], rh.at[0])

    @pl.when(seq == 0)
    def _():
        ext[0] = jnp.zeros((2 * TOK, 6 * HD), BF16)

    @pl.when(seq == n_seq - 1)
    def _():
        ext[5] = jnp.zeros((2 * TOK, 6 * HD), BF16)

    for row in (0, 5):
        for region in range(2):
            rows = pl.ds(region * TOK, TOK)
            put_sides(row, region, ext[row, rows, HD:2 * HD].astype(F32), ext[row, rows, 4 * HD:5 * HD].astype(F32))

    decoded = jnp.dot(lines(0, 4), wide[0], preferred_element_type=F32)
    decoded += jnp.dot(lines(1, 5), wide[1], preferred_element_type=F32)
    decoded += jnp.dot(lines(2, 6), wide[2], preferred_element_type=F32)
    for row in range(PATCH):
        for region in range(2):
            low = (row * 2 + region) * TOK
            for px in range(PATCH):
                grid[region, pl.ds(px, TOK, stride=PATCH), :] = decoded[low:low + TOK, px * HD:(px + 1) * HD]
            dec_ref[region, row] = grid[region].astype(BF16)

    mine = offset // 3
    owns = jnp.logical_and(offset % 3 == 0, mine < OWNED)

    @pl.when(owns)
    def _():
        wait_bytes(buf3.at[pl.ds(0, OWNED - 1)], s3)
        wait_bytes(buf3.at[pl.ds(0, n_yz - 1)], r3)
        buf3[member] = acc2[mine // 2, mine % 2]
        total = jnp.sum(buf3[...], axis=0) * (1.0 / math.sqrt(PATCH * PATCH * TOK))
        fin[mine // 2, mine % 2] = total.astype(BF16)
        part = fin.at[mine // 2, mine % 2]

        def spread(step, _):
            remote(part, part, s4, r4, yz_device((member + step) % n_yz)).start()
            return 0

        lax.fori_loop(1, n_yz, spread, 0)
        wait_bytes(buf4.at[pl.ds(0, n_yz - 1)], s4)
        wait_bytes(buf4.at[pl.ds(0, OWNED - 1)], r4)

    @pl.when(jnp.logical_not(owns))
    def _():
        wait_bytes(buf3.at[pl.ds(0, OWNED)], s3)
        wait_bytes(buf4.at[pl.ds(0, OWNED)], r4)

    def place(which):
        return whole.at[:, pl.ds(8 * core + 2 * which, 2)]

    copies = []
    for step in range(1, X):
        copy = remote(fin, place(x), s5.at[step - 1], r5.at[step - 1], x_device(step))
        copy.start()
        copies.append(copy)
    whole[:, pl.ds(8 * core + 2 * x, 2)] = fin[...]
    forwards = [remote(fin, place(x), s6.at[0], r6.at[0], partner)]
    forwards[0].start()
    for step in range(1, X):
        copies[step - 1].wait()
        block = place((x + X - step) % X)
        forward = remote(block, block, s6.at[step], r6.at[step], partner)
        forward.start()
        forwards.append(forward)

    for copy in x_copies:
        copy.wait_send()
    for array in range(3):
        wait_bytes(landed[array], sz.at[array])
    wait_bytes(o_in, so)
    wait_bytes(att.at[pl.ds(0, 6)], sx2)
    for forward in forwards:
        forward.wait()
    wg_ref[...] = whole[...].astype(F32)


def body(query_rows, key_rows, value_rows, region_lengths, norm_gain, conv_weight, cotangent):
    n_dp = lax.axis_size("dp")
    n_yz = (n_dp // 2) * Z
    hbm = pl.BlockSpec(memory_space=pl.ANY)
    vmem = pl.BlockSpec(memory_space=pltpu.VMEM)
    dma = pltpu.SemaphoreType.DMA
    decoded, grad = pl.pallas_call(
        functools.partial(step_kernel, n_dp),
        out_shape=(jax.ShapeDtypeStruct((2, 4, 256, 128), BF16), jax.ShapeDtypeStruct((9, 16, 8, 128), F32)),
        in_specs=[pl.BlockSpec(memory_space=pltpu.SMEM), hbm, hbm, hbm, vmem, hbm, hbm],
        out_specs=(vmem, vmem),
        scratch_shapes=[
            pltpu.VMEM((3, TOK, 2, HEADS * HD), BF16),
            pltpu.VMEM((9, HD, HD), BF16),
            pltpu.VMEM((2, PATCH, PATCH * TOK, HD), BF16),
            pltpu.VMEM((2, 2, PATCH * TOK, HD), BF16),
            pltpu.VMEM((4, 2 * TOK, HD), F32),
            pltpu.VMEM((3, Z, X, TOK, HD), BF16),
            pltpu.VMEM((3, Z, X, TOK, HD), BF16),
            pltpu.VMEM((Z, X, TOK, HD), BF16),
            pltpu.VMEM((Z, X, TOK, HD), BF16),
            pltpu.VMEM((Z, X, TOK, HD), BF16),
            pltpu.VMEM((3, X, TOK, HD), BF16),
            pltpu.VMEM((Z, X * TOK, X * Z * TOK), BF16),
            pltpu.VMEM((Z, X * TOK, 1), F32),
            pltpu.VMEM((Z, X, TOK, HD), BF16),
            pltpu.VMEM((Z, X, TOK, HD), BF16),
            pltpu.VMEM((X, TOK, HD), BF16),
            pltpu.VMEM((Z, X, TOK, HD), BF16),
            pltpu.VMEM((6, 2 * TOK, 6 * HD), BF16),
            pltpu.VMEM((4 * HD, 6 * 2 * TOK), BF16),
            pltpu.VMEM((2, PATCH * TOK, HD), F32),
            pltpu.VMEM((3, 6 * HD, 4 * HD), BF16),
            pltpu.VMEM((9, 16, 8, HD), F32),
            pltpu.VMEM((9, 8, 8, HD), F32),
            pltpu.VMEM((9, 8, 8, HD), F32),
            pltpu.VMEM((3, 9, 2, 8, HD), F32),
            pltpu.VMEM((9, 2, 8, HD), F32),
            pltpu.VMEM((n_yz, 8, HD), F32),
            pltpu.VMEM((n_yz, 8, HD), BF16),
            pltpu.VMEM((9, 2, 8, HD), BF16),
            pltpu.VMEM((9, 16, 8, HD), BF16),
            dma((5,)), dma((3, 3)), dma((3, 3)), dma((3,)), dma((2,)), dma((7,)), dma((3, X)),
            dma, dma, dma((X,)), dma, dma((8, 3)), dma((2,)), dma((2,)), dma((2,)), dma((2,)),
            dma((3,)), dma((3,)), dma((3, 3)), dma((3, 3)), dma, dma, dma, dma, dma((3,)), dma((3,)), dma((4,)), dma((4,)),
        ],
        compiler_params=pltpu.CompilerParams(
            collective_id=0, has_side_effects=True, vmem_limit_bytes=60 * 1024 * 1024
        ),
        name="region_step",
    )(
        region_lengths,
        query_rows,
        key_rows,
        value_rows,
        norm_gain.reshape(HEADS, HD),
        conv_weight,
        cotangent,
    )
    return decoded, grad.reshape(9, 128, 128)


def solution(mesh):
    placed = (
        P("seq", "dp", None),
        P("seq", "dp", None),
        P("seq", "dp", None),
        P("dp"),
        P(),
        P(),
        P("dp", "seq", None, None),
    )
    return jax.shard_map(
        body,
        mesh=mesh,
        in_specs=placed,
        out_specs=(P("dp", "seq", None, None), P()),
        check_vma=False,
    )
```

time: 129 us -> 110 us (0.85)
  Pallas kernels: 120 us -> 106 us
  local copies, waits for them, and re-layouts: 7.86 us -> 2.75 us
    pallas_call x1, Pallas kernels: 120 us -> 106 us  [body(): pl.pallas_call(functools.partial(step_kernel, n_dp), out_shape=(jax.Shape...]
    reshape x6 -> x0, local copies, waits for them, and re-layouts: 5.03 us -> none  [items(): rows.reshape(TOK, X * Z, HD).transpose(1, 0, 2).reshape(Z, X, TOK, HD)]
    unnamed x8 -> x4, local copies, waits for them, and re-layouts: 2.83 us -> 2.75 us
where the time goes in v3:
time: 110 us
  Pallas kernels  106 us (96%)
  local copies, waits for them, and re-layouts  2.75 us (2%)
    pallas_call x1, Pallas kernels, body(): pl.pallas_call(functools.partial(step_kernel, n_dp), out_shape=(jax.Shape...  106 us
    unnamed x4, local copies, waits for them, and re-layouts  2.75 us

profile of v3, /device:TPU:1, one launch (start us, length us, event | category | flops | bytes accessed | tf_op | source)
XLA Modules:
  0.0 109.6 jit_solution(9576799582865657971)
XLA Ops:
  0.6 106.2 %region_step.1 = (bf16[2,4,256,128]{3,2,1,0:T(8,128)(2,1)}, f32[9,16,8,128]{3,2,1,0:T(8,128)}) custom-call(s32[2]{0:T(128)} %lens_ref.1, bf16[64,2,2048]{2,1,0:T(2,128)(2,1)} %q_hbm.1, bf16[64,2,2048]{2,1,0:T(2,128)(2,1)} %k_hbm.1, bf16[64,2,2048]{2,1,0:T(2,128)(2,1)} %v_hbm.1, f32[16,128]{1,0:T(8,128)} %bitcast.3, bf16[9,128,128]{2,1,0:T(8,128)(2,1)} %w_hbm.1, ...), custom_call_target="tpu_custom_call" | custom-call | tf_op jit(solution)/shard_map/region_step/pallas_call | solution.py:452
  106.8 0.0 copy-start
  106.8 1.9 %copy.11 = bf16[2,4,256,128]{3,2,1,0:T(8,128)(2,1)} copy(bf16[2,4,256,128]{3,2,1,0:T(8,128)(2,1)} %get-tuple-element.8) | data formatting | bytes 1048576
  108.7 0.0 copy-done
  108.8 0.8 copy.12
Async XLA Ops:
  106.8 1.9 %copy-start = (f32[9,16,8,128]{3,2,1,0:T(8,128)S(1)}, f32[9,16,8,128]{3,2,1,0:T(8,128)}, u32[]{:S(2)}) copy-start(f32[9,16,8,128]{3,2,1,0:T(8,128)} %get-tuple-element.5) | copy-start | bytes 1769476

commit v4 on v3

--- a/solution.py
+++ b/solution.py
@@ -30,7 +30,7 @@
 def step_kernel(n_dp, lens_ref, q_hbm, k_hbm, v_hbm, gain_ref, w_hbm, cot_hbm, dec_ref, wg_ref,
                 raw, w_ref, cot_ref, cot_side, pairs, split, stage, rk, rq, rv, hold, probs, sums, o_mid, o_in, o_hold, att, ext, cot_t, grid, wide,
                 taps, buf1, acc1, buf2, acc2, buf3, buf4, fin, whole,
-                load, sx, rx, sz, rz, rzq, rr, so, ro, rro, sx2, rx2, sh, rh, sc, rc,
+                inside, load, sx, rx, sz, rz, rzq, rr, so, ro, rro, sx2, rx2, sh, rh, sc, rc,
                 s1, r1, s2, r2, s3, r3, s4, r4, s5, r5, s6, r6):
     dp, seq = lax.axis_index("dp"), lax.axis_index("seq")
     n_seq = X * Z
@@ -59,18 +59,22 @@
     def signal(device):
         pl.semaphore_signal(barrier, inc=1, device_id=device, device_id_type=MESH)
 
-    def greet(step, _):
-        signal(yz_device((member + step) % n_yz))
-        return 0
-
+    n_y = n_dp // 2
+
+    def y_device(step):
+        return (((dp // 2 + step) % n_y) * 2 + core, seq)
+
+    for step in range(1, n_y):
+        signal(y_device(step))
+    for step in range(1, Z):
+        signal(z_device(step))
     for step in range(1, X):
         signal(x_device(step))
-    lax.fori_loop(1, n_yz, greet, 0)
     signal(partner)
     signal((dp, (seq + 1) % n_seq))
     signal((dp, (seq + n_seq - 1) % n_seq))
 
-    for array in range(3):
+    def divide(array):
         loads[array].wait()
         for head in range(HEADS):
             both = raw[array, :, :, head * HD:(head + 1) * HD].astype(F32)
@@ -78,13 +82,16 @@
             for region in range(2):
                 item = region * HEADS + head
                 split[array, item // X, item % X] = pairs[head % 4, pl.ds(region, TOK, stride=2), :].astype(BF16)
-    pl.semaphore_wait(barrier, (X - 1) + (n_yz - 1) + 1 + 2)
+
+    divide(0)
+    pl.semaphore_wait(barrier, (n_y - 1) + (Z - 1) + (X - 1) + 1 + 2)
 
     landed = (rk, rq, rv)
     far_first = (4, 3, 5, 2, 6, 1, 7)
 
     x_copies = []
-    for array in range(3):
+
+    def along_x(array):
         for step in (1, 3, 2):
             copy = remote(split.at[array, :, (x + step) % X], stage.at[array, :, x],
                           sx.at[array, step - 1], rx.at[array, step - 1], x_device(step))
@@ -113,9 +120,15 @@
                z_device(half)).start()
 
     for array in range(3):
+        if array:
+            divide(array)
+        along_x(array)
         for step in far_first:
             along_z(array, split.at[array], x, step)
         landed[array][z, x] = split[array, z, x]
+
+    for step in range(1, n_y):
+        pl.semaphore_signal(inside, inc=1, device_id=y_device(step), device_id_type=MESH)
 
     loads[3].wait()
     loads[4].wait()
@@ -241,6 +254,26 @@
         remote(o_hold.at[column], att.at[(z + Z - half) % Z, column], so, ro, z_device(half)).start()
     for step in (1, 7):
         passing(step)
+    @pl.when(seq < n_seq - 1)
+    def _():
+        cot_down.wait_send()
+        wait_bytes(cot_side.at[1], rc.at[1])
+
+    @pl.when(seq > 0)
+    def _():
+        cot_up.wait_send()
+        wait_bytes(cot_side.at[0], rc.at[0])
+
+    @pl.when(seq == 0)
+    def _():
+        cot_side[0] = jnp.zeros((2, PATCH * TOK, HD), BF16)
+
+    @pl.when(seq == n_seq - 1)
+    def _():
+        cot_side[1] = jnp.zeros((2, PATCH * TOK, HD), BF16)
+
+    turn(PATCH, cot_side[1, 0], cot_side[1, 1])
+    turn(-1, cot_side[0, 0], cot_side[0, 1])
     for side in range(1, X):
         wait_bytes(att.at[z, (x + X - side) % X], rx2.at[7, side - 1])
     wait_bytes(att.at[pl.ds(0, Z - 1)], ro)
@@ -276,14 +309,6 @@
     down = remote(ext.at[4, :, middle], ext.at[0, :, middle], sh.at[0], rh.at[0], (dp, (seq + 1) % n_seq))
     up = remote(ext.at[1, :, middle], ext.at[5, :, middle], sh.at[1], rh.at[1], (dp, (seq + n_seq - 1) % n_seq))
 
-    @pl.when(seq < n_seq - 1)
-    def _():
-        down.start()
-
-    @pl.when(seq > 0)
-    def _():
-        up.start()
-
     def lines(low, high):
         return ext[low:high].reshape((high - low) * 2 * TOK, 6 * HD)
 
@@ -316,33 +341,23 @@
     taps_of(1)
     to_core(1).start()
 
-    @pl.when(seq < n_seq - 1)
-    def _():
-        cot_down.wait_send()
-        wait_bytes(cot_side.at[1], rc.at[1])
-
-    @pl.when(seq > 0)
-    def _():
-        cot_up.wait_send()
-        wait_bytes(cot_side.at[0], rc.at[0])
-
-    @pl.when(seq == 0)
-    def _():
-        cot_side[0] = jnp.zeros((2, PATCH * TOK, HD), BF16)
-
-    @pl.when(seq == n_seq - 1)
-    def _():
-        cot_side[1] = jnp.zeros((2, PATCH * TOK, HD), BF16)
-
-    turn(PATCH, cot_side[1, 0], cot_side[1, 1])
     taps_of(0)
     to_core(0).start()
     cores_done(1)
-    turn(-1, cot_side[0, 0], cot_side[0, 1])
     taps_of(2)
     to_core(2).start()
     cores_done(0)
     cores_done(2)
+
+    @pl.when(seq < n_seq - 1)
+    def _():
+        down.start()
+
+    @pl.when(seq > 0)
+    def _():
+        up.start()
+
+    pl.semaphore_wait(inside, n_y - 1)
     for dy in (1, 0, 2):
         for step in range(1, X):
             to_x(dy, step).wait()
@@ -451,7 +466,7 @@
     dma = pltpu.SemaphoreType.DMA
     decoded, grad = pl.pallas_call(
         functools.partial(step_kernel, n_dp),
-        out_shape=(jax.ShapeDtypeStruct((2, 4, 256, 128), BF16), jax.ShapeDtypeStruct((9, 16, 8, 128), F32)),
+        out_shape=(pltpu.VMEM((2, 4, 256, 128), BF16), pltpu.VMEM((9, 16, 8, 128), F32)),
         in_specs=[pl.BlockSpec(memory_space=pltpu.SMEM), hbm, hbm, hbm, vmem, hbm, hbm],
         out_specs=(vmem, vmem),
         scratch_shapes=[
@@ -485,7 +500,7 @@
             pltpu.VMEM((n_yz, 8, HD), BF16),
             pltpu.VMEM((9, 2, 8, HD), BF16),
             pltpu.VMEM((9, 16, 8, HD), BF16),
-            dma((5,)), dma((3, 3)), dma((3, 3)), dma((3,)), dma((2,)), dma((7,)), dma((3, X)),
+            pltpu.SemaphoreType.REGULAR, dma((5,)), dma((3, 3)), dma((3, 3)), dma((3,)), dma((2,)), dma((7,)), dma((3, X)),
             dma, dma, dma((X,)), dma, dma((8, 3)), dma((2,)), dma((2,)), dma((2,)), dma((2,)),
             dma((3,)), dma((3,)), dma((3, 3)), dma((3, 3)), dma, dma, dma, dma, dma((3,)), dma((3,)), dma((4,)), dma((4,)),
         ],

time: 110 us -> 104 us (0.945)
  Pallas kernels: 106 us -> 101 us
  local copies, waits for them, and re-layouts: 2.75 us -> 1.61 us
    pallas_call x1, Pallas kernels: 106 us -> 101 us  [body(): pl.pallas_call(functools.partial(step_kernel, n_dp), out_shape=(pltpu.VME...]
    unnamed x4 -> x2, local copies, waits for them, and re-layouts: 2.75 us -> 1.61 us
where the time goes in v4:
time: 104 us
  Pallas kernels  101 us (97%)
  local copies, waits for them, and re-layouts  1.61 us (2%)
    pallas_call x1, Pallas kernels, body(): pl.pallas_call(functools.partial(step_kernel, n_dp), out_shape=(pltpu.VME...  101 us

profile of v4, /device:TPU:1, one launch (start us, length us, event | category | flops | bytes accessed | tf_op | source)
XLA Modules:
  0.0 103.7 jit_solution(10044381846770759401)
XLA Ops:
  0.6 101.5 %region_step.1 = (bf16[2,4,256,128]{3,2,1,0:T(8,128)(2,1)S(1)}, f32[9,16,8,128]{3,2,1,0:T(8,128)S(1)}) custom-call(s32[2]{0:T(128)} %lens_ref.1, bf16[64,2,2048]{2,1,0:T(2,128)(2,1)} %q_hbm.1, bf16[64,2,2048]{2,1,0:T(2,128)(2,1)} %k_hbm.1, bf16[64,2,2048]{2,1,0:T(2,128)(2,1)} %v_hbm.1, f32[16,128]{1,0:T(8,128)} %bitcast.3, bf16[9,128,128]{2,1,0:T(8,128)(2,1)} %w_hbm.1, ...), custom_call_target="tpu_custom_call" | custom-call | tf_op jit(solution)/shard_map/region_step/pallas_call | solution.py:467
  102.1 0.8 copy.11
  102.9 0.8 copy.12

commit v5 on v4

--- a/solution.py
+++ b/solution.py
@@ -314,11 +314,18 @@
 
     def taps_of(dy):
         low = (2 - dy) * 2 * TOK
-        block = jnp.dot(cot_t[:, low:low + PATCH * 2 * TOK], lines(1, 5), preferred_element_type=F32)
+        rows = ext[1:5].reshape(PATCH * 2 * TOK, 6 * HD)
+        blocks = [
+            jnp.dot(cot_t[pair * HD:(pair + 2) * HD, low:low + PATCH * 2 * TOK], rows[:, pair * HD:(pair + 4) * HD],
+                    preferred_element_type=F32)
+            for pair in (0, 2)
+        ]
         for dx in range(3):
-            total = block[0:HD, dx * HD:(dx + 1) * HD]
-            for px in range(1, PATCH):
-                total += block[px * HD:(px + 1) * HD, (px + dx) * HD:(px + dx + 1) * HD]
+            total = None
+            for block in blocks:
+                for px in range(2):
+                    part = block[px * HD:(px + 1) * HD, (px + dx) * HD:(px + dx + 1) * HD]
+                    total = part if total is None else total + part
             taps[3 * dy + dx] = total.T.reshape(16, 8, HD)
 
     def three(ref, dy, *rest):
@@ -406,46 +413,61 @@
 
     mine = offset // 3
     owns = jnp.logical_and(offset % 3 == 0, mine < OWNED)
+    away = [(dy, dz) for dy in range(n_y) for dz in range(Z) if dy or dz]
+    away.sort(key=lambda d: -min(d[0], n_y - d[0]) - min(d[1], Z - d[1]))
 
     @pl.when(owns)
     def _():
-        wait_bytes(buf3.at[pl.ds(0, OWNED - 1)], s3)
         wait_bytes(buf3.at[pl.ds(0, n_yz - 1)], r3)
         buf3[member] = acc2[mine // 2, mine % 2]
         total = jnp.sum(buf3[...], axis=0) * (1.0 / math.sqrt(PATCH * PATCH * TOK))
         fin[mine // 2, mine % 2] = total.astype(BF16)
         part = fin.at[mine // 2, mine % 2]
-
-        def spread(step, _):
-            remote(part, part, s4, r4, yz_device((member + step) % n_yz)).start()
-            return 0
-
-        lax.fori_loop(1, n_yz, spread, 0)
+        for dy, dz in away:
+            device = (((dp // 2 + dy) % n_y) * 2 + core, ((z + dz) % Z) * X + x)
+            remote(part, part, s4, r4.at[mine // 6], device).start()
+
+    def place(dy, which):
+        return whole.at[pl.ds(3 * dy, 3), pl.ds(8 * core + 2 * which, 2)]
+
+    def back_x(dy, step):
+        return remote(three(fin, dy), place(dy, x), s5.at[dy, step - 1], r5.at[dy, step - 1], x_device(step))
+
+    def back_core(dy, number, src, which):
+        return remote(src, place(dy, which), s6.at[dy, number], r6.at[dy, number], partner)
+
+    forwards = []
+    for dy in (1, 0, 2):
+        owned_here = jnp.logical_and(owns, mine // 6 == dy)
+
+        @pl.when(owned_here)
+        def _():
+            wait_bytes(buf4.at[pl.ds(0, 5)], r4.at[dy])
+
+        @pl.when(jnp.logical_not(owned_here))
+        def _():
+            wait_bytes(buf4.at[pl.ds(0, 6)], r4.at[dy])
+
+        for step in (1, 3, 2):
+            back_x(dy, step).start()
+        forwards.append(back_core(dy, 0, three(fin, dy), x))
+        forwards[-1].start()
+        whole[3 * dy:3 * dy + 3, pl.ds(8 * core + 2 * x, 2)] = fin[3 * dy:3 * dy + 3]
+    for dy in (1, 0, 2):
+        for step in (1, 3, 2):
+            back_x(dy, step).wait()
+            which = (x + X - step) % X
+            forwards.append(back_core(dy, step, place(dy, which), which))
+            forwards[-1].start()
+
+    @pl.when(owns)
+    def _():
+        wait_bytes(buf3.at[pl.ds(0, OWNED - 1)], s3)
         wait_bytes(buf4.at[pl.ds(0, n_yz - 1)], s4)
-        wait_bytes(buf4.at[pl.ds(0, OWNED - 1)], r4)
 
     @pl.when(jnp.logical_not(owns))
     def _():
         wait_bytes(buf3.at[pl.ds(0, OWNED)], s3)
-        wait_bytes(buf4.at[pl.ds(0, OWNED)], r4)
-
-    def place(which):
-        return whole.at[:, pl.ds(8 * core + 2 * which, 2)]
-
-    copies = []
-    for step in range(1, X):
-        copy = remote(fin, place(x), s5.at[step - 1], r5.at[step - 1], x_device(step))
-        copy.start()
-        copies.append(copy)
-    whole[:, pl.ds(8 * core + 2 * x, 2)] = fin[...]
-    forwards = [remote(fin, place(x), s6.at[0], r6.at[0], partner)]
-    forwards[0].start()
-    for step in range(1, X):
-        copies[step - 1].wait()
-        block = place((x + X - step) % X)
-        forward = remote(block, block, s6.at[step], r6.at[step], partner)
-        forward.start()
-        forwards.append(forward)
 
     for copy in x_copies:
         copy.wait_send()
@@ -456,6 +478,15 @@
     for forward in forwards:
         forward.wait()
     wg_ref[...] = whole[...].astype(F32)
+
+
+def results_kernel(decoded_ref, grad_ref, decoded_out, grad_out, sems):
+    copies = [pltpu.make_async_copy(decoded_ref, decoded_out, sems.at[0]),
+              pltpu.make_async_copy(grad_ref, grad_out, sems.at[1])]
+    for copy in copies:
+        copy.start()
+    for copy in copies:
+        copy.wait()
 
 
 def body(query_rows, key_rows, value_rows, region_lengths, norm_gain, conv_weight, cotangent):
@@ -502,7 +533,7 @@
             pltpu.VMEM((9, 16, 8, HD), BF16),
             pltpu.SemaphoreType.REGULAR, dma((5,)), dma((3, 3)), dma((3, 3)), dma((3,)), dma((2,)), dma((7,)), dma((3, X)),
             dma, dma, dma((X,)), dma, dma((8, 3)), dma((2,)), dma((2,)), dma((2,)), dma((2,)),
-            dma((3,)), dma((3,)), dma((3, 3)), dma((3, 3)), dma, dma, dma, dma, dma((3,)), dma((3,)), dma((4,)), dma((4,)),
+            dma((3,)), dma((3,)), dma((3, 3)), dma((3, 3)), dma, dma, dma, dma((3,)), dma((3, 3)), dma((3, 3)), dma((3, 4)), dma((3, 4)),
         ],
         compiler_params=pltpu.CompilerParams(
             collective_id=0, has_side_effects=True, vmem_limit_bytes=60 * 1024 * 1024
@@ -517,7 +548,15 @@
         conv_weight,
         cotangent,
     )
-    return decoded, grad.reshape(9, 128, 128)
+    return pl.pallas_call(
+        results_kernel,
+        out_shape=(jax.ShapeDtypeStruct((2, 4, 256, 128), BF16), jax.ShapeDtypeStruct((9, 128, 128), F32)),
+        in_specs=[hbm, hbm],
+        out_specs=(hbm, hbm),
+        scratch_shapes=[dma((2,))],
+        compiler_params=pltpu.CompilerParams(vmem_limit_bytes=2 * 1024 * 1024),
+        name="results",
+    )(decoded, grad.reshape(9, 128, 128))
 
 
 def solution(mesh):

time: 104 us -> 102 us (0.981)
  local copies, waits for them, and re-layouts: 1.61 us -> 0 us
    unnamed x2 -> x0, local copies, waits for them, and re-layouts: 1.61 us -> none
    pallas_call x1, Pallas kernels: 101 us -> 100 us  [body(): pl.pallas_call(functools.partial(step_kernel, n_dp), out_shape=(pltpu.VME...]
where the time goes in v5:
time: 102 us
  Pallas kernels  101 us (99%)
    pallas_call x1, Pallas kernels, body(): pl.pallas_call(functools.partial(step_kernel, n_dp), out_shape=(pltpu.VME...  100 us

profile of v5, /device:TPU:1, one launch (start us, length us, event | category | flops | bytes accessed | tf_op | source)
XLA Modules:
  0.0 102.1 jit_solution(260043412754034330)
XLA Ops:
  0.6 100.3 %region_step.1 = (bf16[2,4,256,128]{3,2,1,0:T(8,128)(2,1)S(1)}, f32[9,16,8,128]{3,2,1,0:T(8,128)S(1)}) custom-call(s32[2]{0:T(128)} %lens_ref.1, bf16[64,2,2048]{2,1,0:T(2,128)(2,1)} %q_hbm.1, bf16[64,2,2048]{2,1,0:T(2,128)(2,1)} %k_hbm.1, bf16[64,2,2048]{2,1,0:T(2,128)(2,1)} %v_hbm.1, f32[16,128]{1,0:T(8,128)} %bitcast.3, bf16[9,128,128]{2,1,0:T(8,128)(2,1)} %w_hbm.1, ...), custom_call_target="tpu_custom_call" | custom-call | tf_op jit(solution)/shard_map/region_step/pallas_call | solution.py:498
  101.0 1.0 results.1

commit v6 on v5

--- a/solution.py
+++ b/solution.py
@@ -51,8 +51,7 @@
 
     loads = [pltpu.make_async_copy(src, dst, load.at[i]) for i, (src, dst) in enumerate((
         (k_hbm, raw.at[0]), (q_hbm, raw.at[1]), (v_hbm, raw.at[2]), (cot_hbm, cot_ref), (w_hbm, w_ref)))]
-    for copy in loads:
-        copy.start()
+    loads[0].start()
 
     barrier = pltpu.get_barrier_semaphore()
 
@@ -76,6 +75,9 @@
 
     def divide(array):
         loads[array].wait()
+        if array == 0:
+            for copy in loads[1:]:
+                copy.start()
         for head in range(HEADS):
             both = raw[array, :, :, head * HD:(head + 1) * HD].astype(F32)
             pairs[head % 4] = both.reshape(2 * TOK, HD)

time: 102 us -> 102 us (level)
  no operation moved by 1% of the time
where the time goes in v6:
time: 102 us
  Pallas kernels  101 us (99%)
    pallas_call x1, Pallas kernels, body(): pl.pallas_call(functools.partial(step_kernel, n_dp), out_shape=(pltpu.VME...  100 us

profile of v6, /device:TPU:1, one launch (start us, length us, event | category | flops | bytes accessed | tf_op | source)
XLA Modules:
  0.0 102.1 jit_solution(15796364322156860556)
XLA Ops:
  0.6 100.3 %region_step.1 = (bf16[2,4,256,128]{3,2,1,0:T(8,128)(2,1)S(1)}, f32[9,16,8,128]{3,2,1,0:T(8,128)S(1)}) custom-call(s32[2]{0:T(128)} %lens_ref.1, bf16[64,2,2048]{2,1,0:T(2,128)(2,1)} %q_hbm.1, bf16[64,2,2048]{2,1,0:T(2,128)(2,1)} %k_hbm.1, bf16[64,2,2048]{2,1,0:T(2,128)(2,1)} %v_hbm.1, f32[16,128]{1,0:T(8,128)} %bitcast.3, bf16[9,128,128]{2,1,0:T(8,128)(2,1)} %w_hbm.1, ...), custom_call_target="tpu_custom_call" | custom-call | tf_op jit(solution)/shard_map/region_step/pallas_call | solution.py:500
  100.9 1.0 results.1
